TPU v7x, 512 devices: a whole 4x4x16 slice. The times are simulated.
512 devices in a mesh: dp: 16 (over z), gy: 4 (over y_lo, core), gz: 8 (over x, y_hi).
Axes of the slice: x: 4, y: 4 (y_hi: 2, y_lo: 2; y = y_hi * 2 + y_lo), z: 16, core: 2. Of those that a mesh axis runs over, the one named last changes fastest.
Arguments:
- volume: bfloat16 [16, 4, 16, 128, 128], P('dp', None, 'gy', 'gz'), may hold values from -6 to 6
- pooled_first: bfloat16 [16, 16, 8, 64, 64], P('dp', None, 'gy', 'gz'), may hold values from -6 to 6
- where_first: int32 [16, 16, 8, 64, 64], P('dp', None, 'gy', 'gz'), may hold values from 0 to 7
- pooled_second: bfloat16 [16, 32, 4, 32, 32], P('dp', None, 'gy', 'gz'), may hold values from -6 to 6
- where_second: int32 [16, 32, 4, 32, 32], P('dp', None, 'gy', 'gz'), may hold values from 0 to 7
- upstream: bfloat16 [16, 32, 4, 32, 32], P('dp', None, 'gy', 'gz'), may hold values from -6 to 6
- kernel_first: bfloat16 [16, 4, 3, 3, 3], replicated, may hold values from -0.625 to 0.625
- kernel_second: bfloat16 [32, 16, 3, 3, 3], replicated, may hold values from -0.3125 to 0.3125
Outputs:
- grad_volume: bfloat16 [16, 4, 16, 128, 128], P('dp', None, 'gy', 'gz')
- grad_kernel_first: float32 [1728], P('dp')
- grad_kernel_second: float32 [13824], P('dp')
All inputs are finite; a program needn't handle non-finite values.
Results may differ from a plain program's by a relative error of at most 0.005.
Values may be sent and summed in bfloat16 or wider, within the bound.
A program may use at most 64 MiB of HBM per device.

v0:
```python
import math

import jax
import jax.numpy as jnp
from jax import lax
from jax.sharding import PartitionSpec as P

leak_rate = 0.3


def extended(block, sides, width):
    for axis, dim in sides:
        count = lax.axis_size(axis)
        forward = [(i, i + 1) for i in range(count - 1)]
        backward = [(target, source) for source, target in forward]
        low = lax.ppermute(
            lax.slice_in_dim(block, block.shape[dim] - width, None, axis=dim), axis, forward
        )
        high = lax.ppermute(lax.slice_in_dim(block, 0, width, axis=dim), axis, backward)
        block = jnp.concatenate([low, block, high], axis=dim)
    return block


def slope_of(pre):
    return jnp.where(pre > 0, 1.0, leak_rate).astype(jnp.float32)


def unpool(values, where):
    parts = [jnp.where(where == k, values, jnp.zeros_like(values)) for k in range(8)]
    stacked = jnp.stack(parts, axis=-1)
    b, c, y, z, x = values.shape
    stacked = stacked.reshape(b, c, y, z, x, 2, 2, 2)
    stacked = jnp.transpose(stacked, (0, 1, 2, 5, 3, 6, 4, 7))
    return stacked.reshape(b, c, 2 * y, 2 * z, 2 * x).astype(jnp.bfloat16)


def pad_along_x(field):
    return jnp.pad(field, ((0, 0), (0, 0), (0, 0), (0, 0), (1, 1)))


def input_grad_rimmed(grad_padded, kernel):
    flipped = jnp.transpose(kernel[:, :, ::-1, ::-1, ::-1], (1, 0, 2, 3, 4))
    return lax.conv_general_dilated(
        pad_along_x(grad_padded),
        flipped,
        (1, 1, 1),
        "VALID",
        dimension_numbers=("NCDHW", "OIDHW", "NCDHW"),
        preferred_element_type=jnp.float32,
    )


def contract_cells(grad, source):
    return lax.dot_general(
        grad, source, (((0, 2, 3, 4), (0, 2, 3, 4)), ((), ())), preferred_element_type=jnp.float32
    )


def kernel_grad_source_rims(grad, source_padded):
    b, o, y, z, x = grad.shape
    source_full = pad_along_x(source_padded)
    taps = []
    for ty in range(3):
        for tz in range(3):
            for tx in range(3):
                taps.append(
                    contract_cells(grad, source_full[:, :, ty : ty + y, tz : tz + z, tx : tx + x])
                )
    return jnp.stack(taps, axis=-1).reshape(-1)


def shards(
    volume,
    pooled_first,
    where_first,
    pooled_second,
    where_second,
    upstream,
    kernel_first,
    kernel_second,
):
    grad_pre2 = unpool(upstream.astype(jnp.float32) * slope_of(pooled_second), where_second)
    first_f = pooled_first.astype(jnp.float32)
    input_second = jnp.where(first_f > 0, first_f, leak_rate * first_f).astype(jnp.bfloat16)
    upper_count = input_second.shape[1]
    joined = jnp.concatenate((input_second, grad_pre2), axis=1)
    joined_rim = extended(joined, (("gy", 2), ("gz", 3)), 1)
    input_rim = joined_rim[:, :upper_count]
    grad_pre2_rim = joined_rim[:, upper_count:]
    second_grad = kernel_grad_source_rims(grad_pre2, input_rim)
    grad_pooled = input_grad_rimmed(grad_pre2_rim, kernel_second)
    grad_pre1 = unpool(grad_pooled * slope_of(pooled_first), where_first)
    lower_count = volume.shape[1]
    joined_low = jnp.concatenate((volume, grad_pre1), axis=1)
    joined_low_rim = extended(joined_low, (("gy", 2), ("gz", 3)), 1)
    volume_rim = joined_low_rim[:, :lower_count]
    grad_pre1_rim = joined_low_rim[:, lower_count:]
    first_grad = kernel_grad_source_rims(grad_pre1, volume_rim)
    grad_vol = input_grad_rimmed(grad_pre1_rim, kernel_first).astype(jnp.bfloat16)
    cells_here = volume.shape[0] * volume.shape[2] * volume.shape[3] * volume.shape[4]
    total = cells_here * lax.axis_size("dp") * lax.axis_size("gy") * lax.axis_size("gz")
    first_term = first_grad * math.sqrt(8.0 / total)
    second_term = second_grad * math.sqrt(64.0 / total)
    first_all, second_all = lax.psum((first_term, second_term), ("gy", "gz"))
    first_out, second_out = (
        lax.psum_scatter(first_all, "dp", scatter_dimension=0, tiled=True),
        lax.psum_scatter(second_all, "dp", scatter_dimension=0, tiled=True),
    )
    return (grad_vol, first_out, second_out)


def solution(mesh):
    placed = (
        P("dp", None, "gy", "gz", None),
        P("dp", None, "gy", "gz", None),
        P("dp", None, "gy", "gz", None),
        P("dp", None, "gy", "gz", None),
        P("dp", None, "gy", "gz", None),
        P("dp", None, "gy", "gz", None),
        P(),
        P(),
    )
    return jax.shard_map(
        shards,
        mesh=mesh,
        in_specs=placed,
        out_specs=(P("dp", None, "gy", "gz", None), P("dp"), P("dp")),
        check_vma=False,
    )
```

profile of v0, /device:TPU:1, one launch (start us, length us, event | category | flops | bytes accessed | tf_op | source)
XLA Modules:
  0.0 362.4 jit_solution(8084981093250992020)
XLA Ops:
  0.7 0.9 fusion.60
  1.6 0.9 constant_dynamic-update-slice_fusion.7
  2.5 0.9 constant_dynamic-update-slice_fusion.6
  3.4 0.9 constant_dynamic-update-slice_fusion.5
  4.3 0.9 constant_dynamic-update-slice_fusion.4
  5.2 0.9 constant_dynamic-update-slice_fusion.3
  6.2 0.9 constant_dynamic-update-slice_fusion.2
  7.1 0.9 constant_dynamic-update-slice_fusion.1
  8.0 0.9 constant_dynamic-update-slice_fusion
  9.3 4.6 %collective-permute-start = (bf16[1,48,1,8,64]{4,1,3,2,0:T(8,128)(2,1)S(1)}, bf16[1,48,1,8,64]{4,1,3,2,0:T(8,128)(2,1)S(1)}, u32[]{:S(2)}, u32[]{:S(2)}) collective-permute-start(bf16[1,48,1,8,64]{4,1,3,2,0:T(8,128)(2,1)S(1)} %get-tuple-element.24), channel_id=1, source_target_pairs={{0,8},{8,16},{16,24},{1,9},{9,17},{17,25},{2,10},{10,18},{18,26},{... | collective-permute-start | bytes 147464 | tf_op jit(solution)/shard_map/ppermute | solution.py:16
  13.9 5.5 %collective-permute-start.1 = (bf16[1,48,1,8,64]{4,1,3,2,0:T(8,128)(2,1)S(1)}, bf16[1,48,1,8,64]{4,1,3,2,0:T(8,128)(2,1)S(1)}, u32[]{:S(2)}, u32[]{:S(2)}) collective-permute-start(bf16[1,48,1,8,64]{4,1,3,2,0:T(8,128)(2,1)S(1)} %get-tuple-element.25), channel_id=1, source_target_pairs={{8,0},{16,8},{24,16},{9,1},{17,9},{25,17},{10,2},{18,10},{26,18},{... | collective-permute-start | bytes 147464 | tf_op jit(solution)/shard_map/ppermute | solution.py:19
  19.4 0.9 collective-permute-done.1
  20.3 4.1 %collective-permute-start.2 = (bf16[1,48,4,1,64]{4,1,3,2,0:T(8,128)(2,1)S(1)}, bf16[1,48,4,1,64]{4,1,3,2,0:T(8,128)(2,1)S(1)}, u32[]{:S(2)}, u32[]{:S(2)}) collective-permute-start(bf16[1,48,4,1,64]{4,1,3,2,0:T(8,128)(2,1)S(1)} %get-tuple-element.20), channel_id=1, source_target_pairs={{0,1},{1,2},{2,3},{3,4},{4,5},{5,6},{6,7},{8,9},{9,10},{10,11},{11... | collective-permute-start | bytes 73736 | tf_op jit(solution)/shard_map/ppermute | solution.py:16
  24.4 1.3 collective-permute-start.3
  25.7 1.3 dynamic-slice
  28.4 2.4 collective-permute-done.3
  38.5 1.1 convolution_select_fusion
  41.2 1.5 copy.264
  42.7 0.8 copy.266
  43.6 2.7 collective-permute-start.4
  46.2 1.9 collective-permute-start.5
  49.1 3.0 collective-permute-done.5
  52.2 5.3 %collective-permute-start.6 = (bf16[1,20,6,1,128]{4,1,3,2,0:T(8,128)(2,1)S(1)}, bf16[1,20,6,1,128]{4,1,3,2,0:T(8,128)(2,1)S(1)}, u32[]{:S(2)}, u32[]{:S(2)}) collective-permute-start(bf16[1,20,6,1,128]{4,1,3,2,0:T(8,128)(2,1)S(1)} %get-tuple-element.18), channel_id=1, source_target_pairs={{0,1},{1,2},{2,3},{3,4},{4,5},{5,6},{6,7},{8,9},{9,10},{10,11},{11... | collective-permute-start | bytes 92168 | tf_op jit(solution)/shard_map/ppermute | solution.py:16
  57.5 1.5 collective-permute-start.7
  60.0 3.7 %collective-permute-done.7 = bf16[1,20,6,1,128]{4,1,3,2,0:T(8,128)(2,1)S(1)} collective-permute-done((bf16[1,20,6,1,128]{4,1,3,2,0:T(8,128)(2,1)S(1)}, bf16[1,20,6,1,128]{4,1,3,2,0:T(8,128)(2,1)S(1)}, u32[]{:S(2)}, u32[]{:S(2)}) %collective-permute-start.7) | collective-permute-done | bytes 30752 | tf_op jit(solution)/shard_map/ppermute | solution.py:19
  77.6 3.9 %reshape.431 = bf16[16,6,18,1,8,17]{5,4,0,2,1,3:T(8,128)(2,1)} reshape(bf16[16,6,18,1,136]{4,0,2,1,3:T(8,128)(2,1)S(1)} %pad.16) | data formatting | bytes 940032 | tf_op jit(solution)/shard_map/conv_general_dilated | solution.py:43
  81.5 8.4 %copy.268 = bf16[16,6,18,1,8,17]{0,4,5,2,1,3:T(8,128)(2,1)} copy(bf16[16,6,18,1,8,17]{5,4,0,2,1,3:T(8,128)(2,1)} %reshape.431) | data formatting | bytes 940032 | tf_op jit(solution)/shard_map/conv_general_dilated | solution.py:43
  89.8 1.1 slice.328
  91.0 138.5 %fusion.3 = bf16[4,16,8,17,4]{2,4,3,1,0:T(4,128)(2,1)S(1)} fusion(bf16[16,4,3,3,3]{0,1,4,3,2:T(4,128)(2,1)S(1)} %copy-done.6, bf16[16,6,18,1,7,2]{0,4,5,2,1,3:T(8,128)(2,1)S(1)} %slice.328, bf16[16,6,18,1,8,17]{0,4,5,2,1,3:T(8,128)(2,1)} %copy.268), kind=kOutput, calls=%fused_computation.4 | convolution fusion | flops 31656960 | bytes 591488 | tf_op jit(solution)/shard_map/conv_general_dilated | solution.py:43
  229.5 1.8 copy.269
  232.5 48.2 %all-reduce.5 = (f32[1728]{0:T(1024)S(1)}, f32[13824]{0:T(1024)S(1)}) all-reduce(f32[1728]{0:T(1024)S(1)} %mul.36, f32[13824]{0:T(1024)S(1)} %mul.39), channel_id=2, replica_groups=mesh['dp'=16,'gy'=4,'gz'=8] {'dp'}, use_global_device_ids=true, to_apply=%region_1.2.clone | all-reduce | flops 15552 | bytes 124416
  280.9 81.2 %all-reduce.4 = (f32[108]{0:T(128)}, f32[864]{0:T(1024)}) all-reduce(f32[108]{0:T(128)S(1)} %dynamic-slice.1, f32[864]{0:T(1024)S(1)} %dynamic-slice.3), channel_id=1, replica_groups=mesh['dp'=16,'gy'=4,'gz'=8] {'gy','gz'}, use_global_device_ids=true, to_apply=%region_0.1 | all-reduce | flops 972 | bytes 7776 | tf_op jit(solution)/shard_map/psum | solution.py:104
  (144 shorter events, 26.8 us)
Async XLA Ops:
  0.6 37.9 %copy-start = (bf16[32,16,3,3,3]{0,1,4,3,2:T(8,128)(2,1)S(1)}, bf16[32,16,3,3,3]{0,1,4,3,2:T(8,128)(2,1)}, u32[]{:S(2)}) copy-start(bf16[32,16,3,3,3]{0,1,4,3,2:T(8,128)(2,1)} %param.15) | copy-start | bytes 82948
  0.6 27.6 %copy-start.3 = (bf16[1,4,4,16,128]{4,3,2,1,0:T(8,128)(2,1)S(1)}, bf16[1,4,4,16,128]{4,3,2,1,0:T(8,128)(2,1)}, u32[]{:S(2)}) copy-start(bf16[1,4,4,16,128]{4,3,2,1,0:T(8,128)(2,1)} %param.8) | copy-start | bytes 196612
  9.3 10.1 %collective-permute-start = (bf16[1,48,1,8,64]{4,1,3,2,0:T(8,128)(2,1)S(1)}, bf16[1,48,1,8,64]{4,1,3,2,0:T(8,128)(2,1)S(1)}, u32[]{:S(2)}, u32[]{:S(2)}) collective-permute-start(bf16[1,48,1,8,64]{4,1,3,2,0:T(8,128)(2,1)S(1)} %get-tuple-element.24), channel_id=1, source_target_pairs={{0,8},{8,16},{16,24},{1,9},{9,17},{17,25},{2,10},{10,18},{18,26},{... | collective-permute-start | bytes 147464 | tf_op jit(solution)/shard_map/ppermute | solution.py:16
  13.9 6.4 %collective-permute-start.1 = (bf16[1,48,1,8,64]{4,1,3,2,0:T(8,128)(2,1)S(1)}, bf16[1,48,1,8,64]{4,1,3,2,0:T(8,128)(2,1)S(1)}, u32[]{:S(2)}, u32[]{:S(2)}) collective-permute-start(bf16[1,48,1,8,64]{4,1,3,2,0:T(8,128)(2,1)S(1)} %get-tuple-element.25), channel_id=1, source_target_pairs={{8,0},{16,8},{24,16},{9,1},{17,9},{25,17},{10,2},{18,10},{26,18},{... | collective-permute-start | bytes 147464 | tf_op jit(solution)/shard_map/ppermute | solution.py:19
  20.3 8.0 %collective-permute-start.2 = (bf16[1,48,4,1,64]{4,1,3,2,0:T(8,128)(2,1)S(1)}, bf16[1,48,4,1,64]{4,1,3,2,0:T(8,128)(2,1)S(1)}, u32[]{:S(2)}, u32[]{:S(2)}) collective-permute-start(bf16[1,48,4,1,64]{4,1,3,2,0:T(8,128)(2,1)S(1)} %get-tuple-element.20), channel_id=1, source_target_pairs={{0,1},{1,2},{2,3},{3,4},{4,5},{5,6},{6,7},{8,9},{9,10},{10,11},{11... | collective-permute-start | bytes 73736 | tf_op jit(solution)/shard_map/ppermute | solution.py:16
  24.4 6.3 %collective-permute-start.3 = (bf16[1,48,4,1,64]{4,1,3,2,0:T(8,128)(2,1)S(1)}, bf16[1,48,4,1,64]{4,1,3,2,0:T(8,128)(2,1)S(1)}, u32[]{:S(2)}, u32[]{:S(2)}) collective-permute-start(bf16[1,48,4,1,64]{4,1,3,2,0:T(8,128)(2,1)S(1)} %get-tuple-element.21), channel_id=1, source_target_pairs={{1,0},{2,1},{3,2},{4,3},{5,4},{6,5},{7,6},{9,8},{10,9},{11,10},{12... | collective-permute-start | bytes 73736 | tf_op jit(solution)/shard_map/ppermute | solution.py:19
  31.6 2.3 copy-start.2
  37.5 1.1 copy-start.7
  39.7 0.9 copy-start.1
  42.7 5.5 %copy-start.4 = (bf16[1,4,4,16,128]{4,3,2,1,0:T(8,128)(2,1)S(1)}, bf16[1,4,4,16,128]{4,3,2,1,0:T(8,128)(2,1)}, u32[]{:S(2)}) copy-start(bf16[1,4,4,16,128]{4,3,2,1,0:T(8,128)(2,1)} %param.8) | copy-start | bytes 196612
  43.6 5.5 %collective-permute-start.4 = (bf16[1,20,1,16,128]{4,1,3,2,0:T(8,128)(2,1)S(1)}, bf16[1,20,1,16,128]{4,1,3,2,0:T(8,128)(2,1)S(1)}, u32[]{:S(2)}, u32[]{:S(2)}) collective-permute-start(bf16[1,20,1,16,128]{4,1,3,2,0:T(8,128)(2,1)S(1)} %get-tuple-element.22), channel_id=1, source_target_pairs={{0,8},{8,16},{16,24},{1,9},{9,17},{17,25},{2,10},{10,18},{18,26},{... | collective-permute-start | bytes 245768 | tf_op jit(solution)/shard_map/ppermute | solution.py:16
  46.2 5.9 %collective-permute-start.5 = (bf16[1,20,1,16,128]{4,1,3,2,0:T(8,128)(2,1)S(1)}, bf16[1,20,1,16,128]{4,1,3,2,0:T(8,128)(2,1)S(1)}, u32[]{:S(2)}, u32[]{:S(2)}) collective-permute-start(bf16[1,20,1,16,128]{4,1,3,2,0:T(8,128)(2,1)S(1)} %get-tuple-element.23), channel_id=1, source_target_pairs={{8,0},{16,8},{24,16},{9,1},{17,9},{25,17},{10,2},{18,10},{26,18},{... | collective-permute-start | bytes 245768 | tf_op jit(solution)/shard_map/ppermute | solution.py:19
  52.2 7.8 %collective-permute-start.6 = (bf16[1,20,6,1,128]{4,1,3,2,0:T(8,128)(2,1)S(1)}, bf16[1,20,6,1,128]{4,1,3,2,0:T(8,128)(2,1)S(1)}, u32[]{:S(2)}, u32[]{:S(2)}) collective-permute-start(bf16[1,20,6,1,128]{4,1,3,2,0:T(8,128)(2,1)S(1)} %get-tuple-element.18), channel_id=1, source_target_pairs={{0,1},{1,2},{2,3},{3,4},{4,5},{5,6},{6,7},{8,9},{9,10},{10,11},{11... | collective-permute-start | bytes 92168 | tf_op jit(solution)/shard_map/ppermute | solution.py:16
  57.5 6.2 %collective-permute-start.7 = (bf16[1,20,6,1,128]{4,1,3,2,0:T(8,128)(2,1)S(1)}, bf16[1,20,6,1,128]{4,1,3,2,0:T(8,128)(2,1)S(1)}, u32[]{:S(2)}, u32[]{:S(2)}) collective-permute-start(bf16[1,20,6,1,128]{4,1,3,2,0:T(8,128)(2,1)S(1)} %get-tuple-element.19), channel_id=1, source_target_pairs={{1,0},{2,1},{3,2},{4,3},{5,4},{6,5},{7,6},{9,8},{10,9},{11,10},{12... | collective-permute-start | bytes 92168 | tf_op jit(solution)/shard_map/ppermute | solution.py:19
  81.5 9.5 %copy-start.6 = (bf16[16,4,3,3,3]{0,1,4,3,2:T(4,128)(2,1)S(1)}, bf16[16,4,3,3,3]{0,1,4,3,2:T(4,128)(2,1)}, u32[]{:S(2)}) copy-start(bf16[16,4,3,3,3]{0,1,4,3,2:T(4,128)(2,1)} %param.14) | copy-start | bytes 10372
  91.0 140.3 %copy-start.5 = (pred[8,17]{1,0:T(8,128)(4,1)S(1)}, pred[8,17]{1,0:T(8,128)(4,1)}, u32[]{:S(2)}) copy-start(pred[8,17]{1,0:T(8,128)(4,1)} %constant.59) | copy-start | bytes 412
where the time goes:
time: 370 us; the launch traced here: 362 us
  matrix products  157 us (42%)
  blocking collectives  129 us (35%)
  starting transfers between devices  26.7 us (7%)
  local copies, waits for them, and re-layouts  26.5 us (7%)
  waiting for transfers between devices  10.1 us (3%)
  other arithmetic  9.83 us (3%)
    conv_general_dilated x2, matrix products, input_grad_rimmed(): lax.conv_general_dilated(pad_along_x(grad_padded), flipped, (1, 1, 1), 'V...  140 us
    psum x1, blocking collectives, shards(): first_all, second_all = lax.psum((first_term, second_term), ('gy', 'gz'))  81.2 us
    unnamed x1, blocking collectives  48.2 us
    dot_general x54, matrix products, contract_cells(): lax.dot_general(grad, source, (((0, 2, 3, 4), (0, 2, 3, 4)), ((), ())), p...  17.5 us
    ppermute x4, starting transfers between devices, extended(): lax.ppermute(lax.slice_in_dim(block, block.shape[dim] - width, None, axis...  16.6 us
    conv_general_dilated x8, local copies, waits for them, and re-layouts, input_grad_rimmed(): lax.conv_general_dilated(pad_along_x(grad_padded), flipped, (1, 1, 1), 'V...  15.5 us
    ppermute x4, starting transfers between devices, extended(): lax.ppermute(lax.slice_in_dim(block, 0, width, axis=dim), axis, backward)  10.1 us
    ppermute x4, waiting for transfers between devices, extended(): lax.ppermute(lax.slice_in_dim(block, 0, width, axis=dim), axis, backward)  10.1 us
  transfers between devices with their start and end apart: 8, of which 4 were waited for; matrix products, arithmetic and copies ran while one was open for 1% of the time, Pallas kernels for 0%

commit v1 on v0

v1 whole, which is shorter than its diff:
```python
import functools
import math

import jax
import jax.numpy as jnp
from jax import lax
from jax.experimental import pallas as pl
from jax.experimental.pallas import tpu as pltpu
from jax.sharding import PartitionSpec as P

MESH = pl.DeviceIdType.MESH
f32, bf16, i32 = jnp.float32, jnp.bfloat16, jnp.int32
LEAK = 0.3
L = 128
NA, NB, NC = 32, 16, 4
HY, HZ = 2, 8
FY, FZ = 4, 16


def iota(shape, dim):
    return lax.broadcasted_iota(i32, shape, dim)


def dot(a, b):
    return lax.dot_general(a, b, (((1,), (0,)), ((), ())), preferred_element_type=f32)


def dot_t(a, b, precision=None):
    return lax.dot_general(
        a, b, (((1,), (1,)), ((), ())), preferred_element_type=f32, precision=precision
    )


def one_hot(mask):
    return jnp.where(mask, 1.0, 0.0).astype(bf16)


def slope_of(pre):
    return jnp.where(pre > 0, 1.0, LEAK).astype(f32)


def moved(value, by):
    lane = iota(value.shape, 1)
    inside = lane >= by if by > 0 else lane < L + by
    return jnp.where(inside, pltpu.roll(value, by % L, 1), 0.0)


def spread_across_x(value, by):
    return [moved(value[:, at : at + L], by) for at in range(0, value.shape[1], L)]


def kernel(
    sizes,
    scales,
    vol,
    first,
    where_first,
    second,
    where_second,
    upstream,
    k1,
    k2,
    grad_vol,
    out,
    g2,
    g1,
    w2,
    w1,
    a3,
    v3,
    s2,
    s1,
    msg,
    rz,
    ry,
    rg,
    sems,
    sem_z,
    sem_y,
    sem_g,
):
    ndp, ngy, ngz = sizes
    dp, gy, gz = lax.axis_index("dp"), lax.axis_index("gy"), lax.axis_index("gz")

    def at(index, step, count):
        return lax.rem(index + (step + count), count)

    def device(d=0, y=0, z=0):
        return {"dp": at(dp, d, ndp), "gy": at(gy, y, ngy), "gz": at(gz, z, ngz)}

    around = [(y, z) for y in (-1, 0, 1) for z in (-1, 0, 1) if (y, z) != (0, 0)]
    partners = [device(d=d) for d in range(1, ndp)]
    partners += [device(y=y, z=z) for y, z in around]
    partners += [device(y=y) for y in range(1, ngy)]
    partners += [device(z=z) for z in range(1, ngz)]
    barrier = pltpu.get_barrier_semaphore()
    for one in partners:
        pl.semaphore_signal(barrier, inc=1, device_id=one, device_id_type=MESH)

    upf = upstream[...].astype(f32)
    e2 = (upf * slope_of(second[...].astype(f32))).astype(bf16).astype(f32)
    p2 = where_second[...].astype(f32)
    quarter = jnp.concatenate(
        [e2[:, z] for z in range(HZ // 2)] + [p2[:, z] for z in range(HZ // 2)], axis=0
    ).astype(bf16)
    by4 = one_hot(iota((L // 4, L), 1) // 4 == iota((L // 4, L), 0))
    quarter = dot(quarter, by4)
    half_x = ((iota((NA, L), 1) // 2) % 2).astype(f32)
    for z in range(HZ // 2):
        e = quarter[z * NA : (z + 1) * NA]
        w = quarter[(HZ // 2 + z) * NA : (HZ // 2 + z + 1) * NA] - half_x
        for dy in range(2):
            for dz in range(2):
                tile = jnp.where(w == 4.0 * dy + 2.0 * dz, e, 0.0).astype(bf16)
                row, col = (2 * z + dz + 1) * NA, (dy + 1) * L
                g2[row : row + NA, col : col + L] = tile

    by2 = one_hot(iota((L // 2, L), 1) // 2 == iota((L // 2, L), 0))
    halves = [first[:, y].astype(f32).reshape(NB * HZ, L // 2) for y in range(HY)]
    halves += [where_first[:, y].astype(f32).reshape(NB * HZ, L // 2) for y in range(HY)]
    halves = [dot(each.astype(bf16), by2).astype(bf16) for each in halves]
    r, s = iota((NB * HZ, NB * HZ), 0), iota((NB * HZ, NB * HZ), 1)
    order = one_hot(s == (r % NB) * HZ + r // NB)
    halves = dot(order, jnp.concatenate(halves, axis=1))
    pre1, p1 = halves[:, : HY * L], halves[:, HY * L :]
    slope1 = slope_of(pre1)
    act = jnp.where(pre1 > 0, pre1, LEAK * pre1).astype(bf16).astype(f32)

    pl.semaphore_wait(barrier, len(partners))

    def exchange(field, chans, ny, nz, base):
        copies = []
        rows = {-1: (0, chans), 0: (chans, nz * chans), 1: ((nz + 1) * chans, chans)}
        cols = {-1: (0, L), 0: (L, ny * L), 1: ((ny + 1) * L, L)}
        for index, (y, z) in enumerate(around):
            row, height = rows[-z]
            col, width = cols[-y]
            from_row = {-1: chans, 0: chans, 1: nz * chans}[z]
            from_col = {-1: L, 0: L, 1: ny * L}[y]
            copy = pltpu.make_async_remote_copy(
                src_ref=field.at[pl.ds(from_row, height), pl.ds(from_col, width)],
                dst_ref=field.at[pl.ds(row, height), pl.ds(col, width)],
                send_sem=sems.at[0, base + index],
                recv_sem=sems.at[1, base + index],
                device_id=device(y=y, z=z),
                device_id_type=MESH,
            )
            copy.start()
            copies.append(copy)
        return copies

    def clear_outside(field, chans, ny, nz):
        height, width = (nz + 2) * chans, (ny + 2) * L
        for on, row, col in (
            (gy == 0, slice(None), slice(0, L)),
            (gy == ngy - 1, slice(None), slice(width - L, width)),
            (gz == 0, slice(0, chans), slice(None)),
            (gz == ngz - 1, slice(height - chans, height), slice(None)),
        ):

            @pl.when(on)
            def _(row=row, col=col):
                field[row, col] = jnp.zeros_like(field[row, col])

    copies2 = exchange(g2, NA, HY, HZ, 0)

    tiled = dot(k2[...], one_hot(iota((NA, (HZ + 2) * NA), 1) % NA == iota((NA, (HZ + 2) * NA), 0)))
    z_of = iota((NB, (HZ + 2) * NA), 1) // NA
    for ty in range(3):
        for tx in range(3):
            for z in range(HZ):
                block = jnp.zeros((NB, (HZ + 2) * NA), f32)
                for tz in range(3):
                    t = ((ty * 3 + tz) * 3 + tx) * NB
                    block = jnp.where(z_of == z - tz + 2, tiled[t : t + NB], block)
                row = ((ty * 3 + tx) * HZ + z) * NB
                w2[row : row + NB, :] = block.astype(bf16)

    for y in range(HY):
        here = act[:, y * L : (y + 1) * L]
        for tx, by in enumerate((2, 0, -2)):
            value = (moved(here, by) if by else here).astype(bf16)
            for z in range(HZ):
                row = (z * 3 + tx) * NB
                a3[row : row + NB, y * L : (y + 1) * L] = value[z * NB : (z + 1) * NB]

    for copy in copies2:
        copy.wait()
    clear_outside(g2, NA, HY, HZ)

    rows2 = 3 * HZ * NB
    total = None
    for ty in range(3):
        part = dot(w2[ty * rows2 : (ty + 1) * rows2, :], g2[:, (2 - ty) * L : (2 - ty + HY) * L])
        total = part if total is None else total + part
    third = HZ * NB
    low = spread_across_x(total[:third], -2)
    high = spread_across_x(total[2 * third :], 2)
    odd_x = (iota((NB, L), 1) % 2).astype(f32)
    for y in range(HY):
        e = total[third : 2 * third, y * L : (y + 1) * L] + low[y] + high[y]
        e = e * slope1[:, y * L : (y + 1) * L]
        w = p1[:, y * L : (y + 1) * L]
        for z in range(HZ):
            ez = e[z * NB : (z + 1) * NB]
            wz = w[z * NB : (z + 1) * NB] - odd_x
            for dy in range(2):
                for dz in range(2):
                    row, col = (2 * z + dz + 1) * NB, (2 * y + dy + 1) * L
                    tile = jnp.where(wz == 4.0 * dy + 2.0 * dz, ez, 0.0).astype(bf16)
                    g1[row : row + NB, col : col + L] = tile

    copies1 = exchange(g1, NB, FY, FZ, 8)

    for ty in range(3):
        taps = None
        for z in range(HZ):
            part = dot_t(
                g2[z * NA : (z + 3) * NA, (2 - ty) * L : (2 - ty + HY) * L],
                a3[z * 3 * NB : (z + 1) * 3 * NB, :],
            )
            taps = part if taps is None else taps + part
        taps = taps * (0.5 * scales[1])
        for tz in range(3):
            row = (ty * 3 + tz) * NA
            s2[row : row + NA, :] = taps[(2 - tz) * NA : (3 - tz) * NA]

    for y in range(FY):
        for i in range(NC):
            here = vol[i, y].astype(f32)
            for tx, by in enumerate((1, 0, -1)):
                row = (tx * NC + i) * FZ
                v3[row : row + FZ, y * L : (y + 1) * L] = (
                    moved(here, by) if by else here
                ).astype(bf16)

    width = (FZ + 2) * NB
    tiled = dot(
        k1[...].astype(f32).reshape(27 * NC, NB).astype(bf16),
        one_hot(iota((NB, width), 1) % NB == iota((NB, width), 0)),
    )
    off = iota((FZ, width), 0) - iota((FZ, width), 1) // NB + 2
    for ty in range(3):
        for tx in range(3):
            for i in range(NC):
                block = jnp.zeros((FZ, width), f32)
                for tz in range(3):
                    t = ((ty * 3 + tz) * 3 + tx) * NC + i
                    line = jnp.broadcast_to(tiled[t : t + 1], (FZ, width))
                    block = jnp.where(off == tz, line, block)
                row = ((ty * 3 + tx) * NC + i) * FZ
                w1[row : row + FZ, :] = block.astype(bf16)

    for copy in copies1:
        copy.wait()
    clear_outside(g1, NB, FY, FZ)

    rows1 = 3 * NC * FZ
    z_of = iota((NB, rows1), 1) % FZ
    groups = jnp.where(iota((NC * 3, rows1), 1) // FZ == iota((NC * 3, rows1), 0), 1.0, 0.0)
    for ty in range(3):
        part = dot_t(g1[:, (2 - ty) * L : (2 - ty + FY) * L], v3[...])
        taps = []
        for tz in range(3):
            tap = jnp.zeros((NB, rows1), f32)
            for z in range(FZ + 2):
                if 0 <= z + tz - 2 < FZ:
                    tap = tap + jnp.where(z_of == z + tz - 2, part[z * NB : (z + 1) * NB], 0.0)
            taps.append(tap)
        taps = jnp.concatenate(taps, axis=0) * scales[0]
        s1[ty * 3 * NB : (ty + 1) * 3 * NB, :] = dot_t(
            taps, groups.astype(f32), lax.Precision.HIGHEST
        )

    msg[...] = jnp.zeros_like(msg)
    wide, per2, per1 = 3 * NB, NA // ndp, NB // ndp
    for k in range(ndp):
        for o in range(per2):
            msg[k, 0:9, o * wide : (o + 1) * wide] = s2[pl.ds(k * per2 + o, 9, stride=NA), :]
        for o in range(per1):
            at_lane = per2 * wide + o * 3 * NC
            msg[k, 0:9, at_lane : at_lane + 3 * NC] = s1[pl.ds(k * per1 + o, 9, stride=NB), :]

    copies_z = []
    for d in range(1, ndp):
        copy = pltpu.make_async_remote_copy(
            src_ref=msg.at[at(dp, d, ndp)],
            dst_ref=rz.at[d],
            send_sem=sem_z.at[0, d],
            recv_sem=sem_z.at[1, d],
            device_id=device(d=d),
            device_id_type=MESH,
        )
        copy.start()
        copies_z.append(copy)

    total = None
    for ty in range(3):
        part = dot(w1[ty * rows1 : (ty + 1) * rows1, :], g1[:, (2 - ty) * L : (2 - ty + FY) * L])
        total = part if total is None else total + part
    third = NC * FZ
    low = spread_across_x(total[:third], -1)
    high = spread_across_x(total[2 * third :], 1)
    for y in range(FY):
        value = total[third : 2 * third, y * L : (y + 1) * L] + low[y] + high[y]
        for i in range(NC):
            grad_vol[i, y] = value[i * FZ : (i + 1) * FZ].astype(bf16)

    for copy in copies_z:
        copy.wait()
    own = msg[dp]
    for d in range(1, ndp):
        own = own + rz[d]

    def shared(value, slots, sem, count, index, where):
        slots[index] = value
        copies = []
        for d in range(1, count):
            copy = pltpu.make_async_remote_copy(
                src_ref=slots.at[index],
                dst_ref=slots.at[index],
                send_sem=sem.at[0, d],
                recv_sem=sem.at[1, d],
                device_id=where(d),
                device_id_type=MESH,
            )
            copy.start()
            copies.append(copy)
        for copy in copies:
            copy.wait()
        value = slots[0]
        for d in range(1, count):
            value = value + slots[d]
        return value

    own = shared(own, ry, sem_y, ngy, gy, lambda d: device(y=d))
    out[...] = shared(own, rg, sem_g, ngz, gz, lambda d: device(z=d))


def shards(sizes, scales, volume, first, where_first, second, where_second, upstream, k1, k2):
    ndp, ngy, ngz = sizes
    k1 = jnp.transpose(k1, (2, 3, 4, 1, 0)).reshape(27, NC, NB)
    k2 = jnp.transpose(k2, (2, 3, 4, 1, 0)).reshape(27 * NB, NA)
    per2, per1 = NA // ndp, NB // ndp
    wide = pl.cdiv((per2 * NB + per1 * NC) * 3, L) * L
    vmem = pl.BlockSpec(memory_space=pltpu.VMEM)
    grad_vol, sums = pl.pallas_call(
        functools.partial(kernel, sizes, scales),
        out_shape=(
            jax.ShapeDtypeStruct((NC, FY, FZ, L), bf16),
            jax.ShapeDtypeStruct((16, wide), f32),
        ),
        in_specs=[vmem] * 8,
        out_specs=(vmem, vmem),
        scratch_shapes=[
            pltpu.VMEM(((HZ + 2) * NA, (HY + 2) * L), bf16),
            pltpu.VMEM(((FZ + 2) * NB, (FY + 2) * L), bf16),
            pltpu.VMEM((9 * HZ * NB, (HZ + 2) * NA), bf16),
            pltpu.VMEM((9 * NC * FZ, (FZ + 2) * NB), bf16),
            pltpu.VMEM((HZ * 3 * NB, HY * L), bf16),
            pltpu.VMEM((3 * NC * FZ, FY * L), bf16),
            pltpu.VMEM((9 * NA, 3 * NB), f32),
            pltpu.VMEM((9 * NB, 3 * NC), f32),
            pltpu.VMEM((ndp, 16, wide), f32),
            pltpu.VMEM((ndp, 16, wide), f32),
            pltpu.VMEM((ngy, 16, wide), f32),
            pltpu.VMEM((ngz, 16, wide), f32),
            pltpu.SemaphoreType.DMA((2, 16)),
            pltpu.SemaphoreType.DMA((2, ndp)),
            pltpu.SemaphoreType.DMA((2, ngy)),
            pltpu.SemaphoreType.DMA((2, ngz)),
        ],
        compiler_params=pltpu.CompilerParams(collective_id=0, has_side_effects=True),
    )(
        volume[0],
        first[0],
        where_first[0],
        second[0, :, 0],
        where_second[0, :, 0],
        upstream[0, :, 0],
        k1,
        k2,
    )
    sums = sums[:9]
    second_out = sums[:, : per2 * 3 * NB].reshape(3, 3, per2, 3, NB)
    second_out = jnp.transpose(second_out, (2, 4, 0, 1, 3)).reshape(-1)
    first_out = sums[:, per2 * 3 * NB : (per2 * NB + per1 * NC) * 3].reshape(3, 3, per1, 3, NC)
    first_out = jnp.transpose(first_out, (2, 4, 0, 1, 3)).reshape(-1)
    return (grad_vol[None], first_out, second_out)


def solution(mesh):
    sizes = tuple(mesh.shape[axis] for axis in ("dp", "gy", "gz"))
    cells = sizes[0] * sizes[1] * sizes[2] * FY * FZ * L
    scales = (math.sqrt(8.0 / cells), math.sqrt(64.0 / cells))
    split = P("dp", None, "gy", "gz", None)
    return jax.shard_map(
        functools.partial(shards, sizes, scales),
        mesh=mesh,
        in_specs=(split,) * 6 + (P(), P()),
        out_specs=(split, P("dp"), P("dp")),
        check_vma=False,
    )
```

time: 370 us -> 51.6 us (0.14); the launches traced: 362 us -> 51.4 us
  matrix products: 157 us -> 0 us
  blocking collectives: 129 us -> 0 us
  Pallas kernels: 0 us -> 47.2 us
  starting transfers between devices: 26.7 us -> 0 us
  local copies, waits for them, and re-layouts: 26.5 us -> 3.46 us
  waiting for transfers between devices: 10.1 us -> 0 us
  other arithmetic: 9.83 us -> 0 us
    conv_general_dilated x2 -> x0, matrix products: 140 us -> none  [input_grad_rimmed(): lax.conv_general_dilated(pad_along_x(grad_padded), flipped, (1, 1, 1), 'V...]
    psum x1 -> x0, blocking collectives: 81.2 us -> none  [shards(): first_all, second_all = lax.psum((first_term, second_term), ('gy', 'gz'))]
    unnamed x1 -> x0, blocking collectives: 48.2 us -> none
    pallas_call x0 -> x1, Pallas kernels: none -> 47.2 us  [shards(): pl.pallas_call(functools.partial(kernel, sizes, scales), out_shape=(jax.S...]
    ppermute x8 -> x0, starting transfers between devices: 26.7 us -> none  [the longest x4 16.6 us: extended(): lax.ppermute(lax.slice_in_dim(block, block.shape[dim] - width, None, axis...]
    dot_general x54 -> x0, matrix products: 17.5 us -> none  [contract_cells(): lax.dot_general(grad, source, (((0, 2, 3, 4), (0, 2, 3, 4)), ((), ())), p...]
    conv_general_dilated x8 -> x0, local copies, waits for them, and re-layouts: 15.5 us -> none  [input_grad_rimmed(): lax.conv_general_dilated(pad_along_x(grad_padded), flipped, (1, 1, 1), 'V...]
    ppermute x8 -> x0, waiting for transfers between devices: 10.1 us -> none  [the longest x4 10.1 us: extended(): lax.ppermute(lax.slice_in_dim(block, 0, width, axis=dim), axis, backward)]
  transfers between devices with their start and end apart: 8 -> 0, of which waited for: 4 -> 0; matrix products, arithmetic and copies ran while one was open for 1% -> 0% of each run, Pallas kernels for 0% -> 0%
where the time goes in v1:
time: 51.6 us; the launch traced here: 51.4 us
  Pallas kernels  47.2 us (91%)
  local copies, waits for them, and re-layouts  3.46 us (7%)
  between operations  0.66 us (1%)
    pallas_call x1, Pallas kernels, shards(): pl.pallas_call(functools.partial(kernel, sizes, scales), out_shape=(jax.S...  47.2 us

profile of v1, /device:TPU:1, one launch (start us, length us, event | category | flops | bytes accessed | tf_op | source)
XLA Modules:
  0.0 51.4 jit_solution(5829000290031225361)
XLA Ops:
  0.6 47.2 %shard_map.103 = (bf16[4,4,16,128]{3,2,1,0:T(8,128)(2,1)}, f32[16,128]{1,0:T(8,128)}) custom-call(bf16[4,4,16,128]{3,2,1,0:T(8,128)(2,1)} %bitcast.21, bf16[16,2,8,64]{3,2,1,0:T(8,128)(2,1)} %bitcast.22, s32[16,2,8,64]{3,2,1,0:T(8,128)} %bitcast.17, bf16[32,4,32]{2,1,0:T(4,128)(2,1)} %bitcast.24, s32[32,4,32]{2,1,0:T(4,128)} %bitcast.23, ...), custom_call_target="tpu_custom_call" | custom-call | tf_op jit(solution)/shard_map/pallas_call | solution.py:347
  47.9 0.8 %slice.9 = f32[9,12]{1,0:T(8,128)S(1)} slice(f32[16,128]{1,0:T(8,128)} %get-tuple-element.6), slice={[0:9], [96:108]} | slice | bytes 864 | tf_op jit(solution)/shard_map/slice | solution.py:387
  48.7 0.1 reshape.26
  48.7 0.2 copy.12
  48.9 0.0 copy-start.1
  48.9 0.6 %reshape.27 = f32[108]{0:T(128)} reshape(f32[1,4,3,3,3]{4,3,2,1,0:T(4,128)S(1)} %copy.12) | data formatting | bytes 864 | tf_op jit(solution)/shard_map/reshape | solution.py:388
  49.5 0.1 copy-done.1
  49.6 0.1 reshape.28
  49.7 0.2 copy.13
  49.9 0.0 copy-start
  49.9 0.8 %reshape.29 = f32[864]{0:T(1024)} reshape(f32[2,16,3,3,3]{4,3,2,1,0:T(4,128)S(1)} %copy.13) | data formatting | bytes 6912 | tf_op jit(solution)/shard_map/reshape | solution.py:386
  50.7 0.0 copy-done
  50.7 0.6 %copy.15 = bf16[1,4,4,16,128]{4,3,2,1,0:T(8,128)(2,1)} copy(bf16[1,4,4,16,128]{4,3,2,1,0:T(8,128)(2,1)S(1)} %bitcast.20) | data formatting | bytes 131072
Async XLA Ops:
  48.9 0.7 %copy-start.1 = (f32[16,128]{1,0:T(8,128)S(1)}, f32[16,128]{1,0:T(8,128)}, u32[]{:S(2)}) copy-start(f32[16,128]{1,0:T(8,128)} %get-tuple-element.6) | copy-start | bytes 24580
  49.9 0.8 %copy-start = (bf16[4,4,16,128]{3,2,1,0:T(8,128)(2,1)S(1)}, bf16[4,4,16,128]{3,2,1,0:T(8,128)(2,1)}, u32[]{:S(2)}) copy-start(bf16[4,4,16,128]{3,2,1,0:T(8,128)(2,1)} %get-tuple-element.5) | copy-start | bytes 196612

commit v2 on v1

v2 whole, which is shorter than its diff:
```python
import functools
import math

import jax
import jax.numpy as jnp
from jax import lax
from jax.experimental import pallas as pl
from jax.experimental.pallas import tpu as pltpu
from jax.sharding import PartitionSpec as P

MESH = pl.DeviceIdType.MESH
f32, bf16, i32 = jnp.float32, jnp.bfloat16, jnp.int32
LEAK = 0.3
L = 128
NA, NB, NC = 32, 16, 4
HY, HZ = 2, 8
FY, FZ = 4, 16


def iota(shape, dim):
    return lax.broadcasted_iota(i32, shape, dim)


def dot(a, b):
    return lax.dot_general(a, b, (((1,), (0,)), ((), ())), preferred_element_type=f32)


def dot_t(a, b, precision=None):
    return lax.dot_general(
        a, b, (((1,), (1,)), ((), ())), preferred_element_type=f32, precision=precision
    )


def one_hot(mask):
    return jnp.where(mask, 1.0, 0.0).astype(bf16)


def slope_of(pre):
    return jnp.where(pre > 0, 1.0, LEAK).astype(f32)


def moved(value, by):
    lane = iota(value.shape, 1)
    inside = lane >= by if by > 0 else lane < L + by
    return jnp.where(inside, pltpu.roll(value, by % L, 1), 0.0)


def spread_across_x(value, by):
    return [moved(value[:, at : at + L], by) for at in range(0, value.shape[1], L)]


def exactly(value, mask):
    high = value.astype(bf16).astype(f32)
    middle = (value - high).astype(bf16).astype(f32)
    pieces = jnp.concatenate([high, middle, value - high - middle], axis=0).astype(bf16)
    pieces = dot(pieces, mask)
    rows = value.shape[0]
    return pieces[:rows] + pieces[rows : 2 * rows] + pieces[2 * rows :]


def kernel(
    sizes,
    scales,
    vol,
    first,
    where_first,
    second,
    where_second,
    upstream,
    k1,
    k2,
    grad_vol,
    out1,
    out2,
    g2,
    g1,
    w2,
    w1,
    a3,
    v3,
    vf,
    vh,
    s2,
    msg1,
    msg2,
    rz1,
    rz2,
    rp1,
    rp2,
    sem_h,
    sem_z,
    sem_p,
):
    ndp, ngy, ngz = sizes
    per2, per1 = NA // ndp, NB // ndp
    dp, gy, gz = lax.axis_index("dp"), lax.axis_index("gy"), lax.axis_index("gz")

    def at(index, step, count):
        return lax.rem(index + (step + count), count)

    def device(d=0, y=0, z=0):
        return {"dp": at(dp, d, ndp), "gy": at(gy, y, ngy), "gz": at(gz, z, ngz)}

    around = [(y, z) for y in (-1, 0, 1) for z in (-1, 0, 1) if (y, z) != (0, 0)]
    plane = [(y, z) for y in range(ngy) for z in range(ngz) if (y, z) != (0, 0)]

    def exists(y, z):
        on = None
        for step, index, count in ((y, gy, ngy), (z, gz, ngz)):
            if step:
                inside = index > 0 if step < 0 else index < count - 1
                on = inside if on is None else jnp.logical_and(on, inside)
        return on

    for field, chans, ny, nz in ((g2, NA, HY, HZ), (g1, NB, FY, FZ)):
        high, wide = (nz + 1) * chans, (ny + 1) * L
        for row, col in (
            (slice(0, chans), slice(None)),
            (slice(high, high + chans), slice(None)),
            (slice(chans, high), slice(0, L)),
            (slice(chans, high), slice(wide, wide + L)),
        ):
            field[row, col] = jnp.zeros_like(field[row, col])
    rows1 = 3 * NC * FZ
    v3[rows1:, :] = jnp.zeros_like(v3[rows1:, :])
    vh[...] = jnp.zeros_like(vh)
    s2[...] = jnp.zeros_like(s2)

    partners = [device(d=d) for d in range(1, ndp)] + [device(y=y, z=z) for y, z in plane]
    barrier = pltpu.get_barrier_semaphore()
    for one in partners:
        pl.semaphore_signal(barrier, inc=1, device_id=one, device_id_type=MESH)

    upf = upstream[...].astype(f32)
    e2 = (upf * slope_of(second[...].astype(f32))).astype(bf16).astype(f32)
    p2 = where_second[...].astype(f32)
    quarter = jnp.concatenate(
        [e2[:, z] for z in range(HZ // 2)] + [p2[:, z] for z in range(HZ // 2)], axis=0
    ).astype(bf16)
    by4 = one_hot(iota((L // 4, L), 1) // 4 == iota((L // 4, L), 0))
    quarter = dot(quarter, by4)
    half_x = ((iota((NA, L), 1) // 2) % 2).astype(f32)
    for z in range(HZ // 2):
        e = quarter[z * NA : (z + 1) * NA]
        w = quarter[(HZ // 2 + z) * NA : (HZ // 2 + z + 1) * NA] - half_x
        for dy in range(2):
            for dz in range(2):
                tile = jnp.where(w == 4.0 * dy + 2.0 * dz, e, 0.0).astype(bf16)
                row, col = (2 * z + dz + 1) * NA, (dy + 1) * L
                g2[row : row + NA, col : col + L] = tile

    def put_volume(here, i, col):
        for tx, by in enumerate((1, 0, -1)):
            row = (tx * NC + i) * FZ
            v3[row : row + FZ, col : col + L] = (moved(here, by) if by else here).astype(bf16)

    for y in range(FY):
        for i in range(NC):
            put_volume(vol[i, y].astype(f32), i, (y + 1) * L)
    r, c = iota((2 * NB, rows1), 0), iota((2 * NB, rows1), 1)
    sides = one_hot(c == (r % NB) * FZ + (r // NB) * (FZ - 1))
    vf[...] = dot(sides, v3[:rows1, L : (FY + 1) * L]).astype(bf16)

    by2 = one_hot(iota((L // 2, L), 1) // 2 == iota((L // 2, L), 0))
    halves = [first[:, y].astype(f32).reshape(NB * HZ, L // 2) for y in range(HY)]
    halves += [where_first[:, y].astype(f32).reshape(NB * HZ, L // 2) for y in range(HY)]
    halves = [dot(each.astype(bf16), by2).astype(bf16) for each in halves]
    r, c = iota((NB * HZ, NB * HZ), 0), iota((NB * HZ, NB * HZ), 1)
    order = one_hot(c == (r % NB) * HZ + r // NB)
    halves = dot(order, jnp.concatenate(halves, axis=1))
    pre1, p1 = halves[:, : HY * L], halves[:, HY * L :]
    slope1 = slope_of(pre1)
    act = jnp.where(pre1 > 0, pre1, LEAK * pre1).astype(bf16).astype(f32)

    pl.semaphore_wait(barrier, len(partners))

    def remote(src, dst, sems, index, to):
        return pltpu.make_async_remote_copy(
            src_ref=src,
            dst_ref=dst,
            send_sem=sems.at[0, index],
            recv_sem=sems.at[1, index],
            device_id=to,
            device_id_type=MESH,
        )

    def start(copies):
        for side, copy in copies:
            pl.when(exists(*side))(copy.start)

    def finish(copies):
        for (y, z), copy in copies:
            pl.when(exists(y, z))(copy.wait_send)
            pl.when(exists(-y, -z))(copy.wait_recv)

    def rim(field, chans, ny, nz, base):
        copies = []
        inner = {-1: (1, 1), 0: (1, None), 1: (None, 1)}
        for index, (y, z) in enumerate(around):
            height, width = (1 if z else nz), (1 if y else ny)
            from_row, to_row = (nz if z > 0 else 1), {-1: nz + 1, 0: 1, 1: 0}[z]
            from_col, to_col = (ny if y > 0 else 1), {-1: ny + 1, 0: 1, 1: 0}[y]
            source = field.at[
                pl.ds(from_row * chans, height * chans), pl.ds(from_col * L, width * L)
            ]
            target = field.at[
                pl.ds(to_row * chans, height * chans), pl.ds(to_col * L, width * L)
            ]
            copies.append(
                ((y, z), remote(source, target, sem_h, base + index, device(y=y, z=z)))
            )
        return copies

    def volume_rim(base):
        copies = []
        for index, (y, z) in enumerate(around):
            if z == 0:
                source, target = vol.at[:, FY - 1 if y > 0 else 0], vh.at[0 if y > 0 else 1]
            else:
                from_col, to_col = (FY - 1 if y > 0 else 0), {-1: FY + 1, 0: 1, 1: 0}[y]
                width = 1 if y else FY
                from_row, to_row = (NB if z > 0 else 0), rows1 + (0 if z > 0 else NB)
                source = vf.at[pl.ds(from_row, NB), pl.ds(from_col * L, width * L)]
                target = v3.at[pl.ds(to_row, NB), pl.ds(to_col * L, width * L)]
            copies.append(
                ((y, z), remote(source, target, sem_h, base + index, device(y=y, z=z)))
            )
        return copies

    rim2, rim_v = rim(g2, NA, HY, HZ, 0), volume_rim(8)
    start(rim2)
    start(rim_v)

    tiled = dot(k2[...], one_hot(iota((NA, (HZ + 2) * NA), 1) % NA == iota((NA, (HZ + 2) * NA), 0)))
    z_of = iota((NB, (HZ + 2) * NA), 1) // NA
    for ty in range(3):
        for tx in range(3):
            for z in range(HZ):
                block = jnp.zeros((NB, (HZ + 2) * NA), f32)
                for tz in range(3):
                    t = ((ty * 3 + tz) * 3 + tx) * NB
                    block = jnp.where(z_of == z - tz + 2, tiled[t : t + NB], block)
                row = ((ty * 3 + tx) * HZ + z) * NB
                w2[row : row + NB, :] = block.astype(bf16)

    for y in range(HY):
        here = act[:, y * L : (y + 1) * L]
        for tx, by in enumerate((2, 0, -2)):
            value = (moved(here, by) if by else here).astype(bf16)
            for z in range(HZ):
                row = (z * 3 + tx) * NB
                a3[row : row + NB, y * L : (y + 1) * L] = value[z * NB : (z + 1) * NB]

    width = (FZ + 2) * NB
    tiled = dot(
        k1[...].astype(f32).reshape(27 * NC, NB).astype(bf16),
        one_hot(iota((NB, width), 1) % NB == iota((NB, width), 0)),
    )
    off = iota((FZ, width), 0) - iota((FZ, width), 1) // NB + 2
    for ty in range(3):
        for tx in range(3):
            for i in range(NC):
                block = jnp.zeros((FZ, width), f32)
                for tz in range(3):
                    t = ((ty * 3 + tz) * 3 + tx) * NC + i
                    line = jnp.broadcast_to(tiled[t : t + 1], (FZ, width))
                    block = jnp.where(off == tz, line, block)
                row = ((ty * 3 + tx) * NC + i) * FZ
                w1[row : row + FZ, :] = block.astype(bf16)

    finish(rim2)

    for ty in range(3):
        taps = None
        for z in range(HZ):
            part = dot_t(
                g2[z * NA : (z + 3) * NA, (2 - ty) * L : (2 - ty + HY) * L],
                a3[z * 3 * NB : (z + 1) * 3 * NB, :],
            )
            taps = part if taps is None else taps + part
        taps = taps * (0.5 * scales[1])
        for tz in range(3):
            row = (ty * 3 + tz) * NA
            s2[row : row + NA, : 3 * NB] = taps[(2 - tz) * NA : (3 - tz) * NA]

    behind = per2 * 3 * NB
    def part_of_row(row, lane):
        value = s2[pl.ds(row, ndp, stride=per2), :]
        if msg2.shape[1] > L:
            rest = jnp.zeros((ndp, msg2.shape[1] - L), f32)
            value = jnp.concatenate([value, rest], axis=1)
        return pltpu.roll(value, lane, 1) if lane else value

    def masked(value, lane):
        at_lane = iota(value.shape, 1)
        return jnp.where(jnp.logical_and(at_lane >= lane, at_lane < lane + NB), value, 0.0)

    for tap in range(8):
        value = part_of_row(tap * NA, 0)
        for o in range(1, per2):
            value = value + part_of_row(tap * NA + o, o * 3 * NB)
        for piece in range(tap, 3 * per2, 8):
            lane, tx = behind + piece // 8 * NB, piece % 3
            moved_by = (lane - tx * NB) % msg2.shape[1]
            value = value + masked(part_of_row(8 * NA + piece // 3, moved_by), lane)
        msg2[pl.ds(tap, ndp, stride=8), :] = value

    def scatter(message, slots, base):
        copies = []
        for d in range(1, ndp):
            copy = remote(message(at(dp, d, ndp)), slots.at[d], sem_z, base + d, device(d=d))
            copy.start()
            copies.append(copy)
        return copies

    scatter2 = scatter(lambda k: msg2.at[pl.ds(pl.multiple_of(k * 8, 8), 8), :], rz2, 0)

    rows2 = 3 * HZ * NB
    total = None
    for ty in range(3):
        part = dot(w2[ty * rows2 : (ty + 1) * rows2, :], g2[:, (2 - ty) * L : (2 - ty + HY) * L])
        total = part if total is None else total + part
    third = HZ * NB
    low = spread_across_x(total[:third], -2)
    high = spread_across_x(total[2 * third :], 2)
    odd_x = (iota((NB, L), 1) % 2).astype(f32)
    for y in range(HY):
        e = total[third : 2 * third, y * L : (y + 1) * L] + low[y] + high[y]
        e = e * slope1[:, y * L : (y + 1) * L]
        w = p1[:, y * L : (y + 1) * L]
        for z in range(HZ):
            ez = e[z * NB : (z + 1) * NB]
            wz = w[z * NB : (z + 1) * NB] - odd_x
            for dy in range(2):
                for dz in range(2):
                    row, col = (2 * z + dz + 1) * NB, (2 * y + dy + 1) * L
                    tile = jnp.where(wz == 4.0 * dy + 2.0 * dz, ez, 0.0).astype(bf16)
                    g1[row : row + NB, col : col + L] = tile

    rim1 = rim(g1, NB, FY, FZ, 16)
    start(rim1)

    finish(rim_v)
    for side in range(2):
        for i in range(NC):
            put_volume(vh[side, i].astype(f32), i, side * (FY + 1) * L)

    count = rows1 + 2 * NB
    c = iota((NB, count), 1)
    z_of = jnp.where(c < rows1, c % FZ, jnp.where(c < rows1 + NB, -1, FZ))
    r, c = iota((count, L), 0), iota((count, L), 1)
    q = jnp.where(r < rows1, r // FZ, (r - rows1) % NB)
    lanes = one_hot(jnp.logical_and(q < 3 * NC, c == (q % NC) * 27 + q // NC))
    line = None
    for ty in range(3):
        part = dot_t(g1[NB : (FZ + 1) * NB, L : (FY + 1) * L], v3[:, ty * L : (ty + FY) * L])
        taps = []
        for tz in range(3):
            tap = None
            for z in range(FZ):
                add = jnp.where(z_of == z + tz - 1, part[z * NB : (z + 1) * NB], 0.0)
                tap = add if tap is None else tap + add
            taps.append(tap)
        taps = exactly(jnp.concatenate(taps, axis=0) * scales[0], lanes)
        for tz in range(3):
            tap = taps[tz * NB : (tz + 1) * NB]
            shift = (ty * 3 + tz) * 3
            tap = pltpu.roll(tap, shift, 1) if shift else tap
            line = tap if line is None else line + tap
    for k in range(ndp):
        for o in range(per1):
            row = k * per1 + o
            msg1[k, :, o * L : (o + 1) * L] = line[row : row + 1]

    scatter1 = scatter(lambda k: msg1.at[k], rz1, ndp)

    finish(rim1)

    total = None
    for ty in range(3):
        part = dot(w1[ty * rows1 : (ty + 1) * rows1, :], g1[:, (2 - ty) * L : (2 - ty + FY) * L])
        total = part if total is None else total + part
    third = NC * FZ
    low = spread_across_x(total[:third], -1)
    high = spread_across_x(total[2 * third :], 1)
    for y in range(FY):
        value = total[third : 2 * third, y * L : (y + 1) * L] + low[y] + high[y]
        for i in range(NC):
            grad_vol[i, y] = value[i * FZ : (i + 1) * FZ].astype(bf16)

    wide2 = pl.cdiv(out2.shape[0], L) * L
    r, c = iota((msg2.shape[1], wide2), 0), iota((msg2.shape[1], wide2), 1)
    of_row = (r // (3 * NB) * NB + r % NB) * 27 + r % (3 * NB) // NB
    to_main = one_hot(jnp.logical_and(r < behind, c == of_row))
    to_last = [
        one_hot(jnp.logical_and((r - behind) // NB == group, c == r % NB * 27))
        for group in range(pl.cdiv(3 * per2, 8))
    ]

    here = gy * ngz + gz

    def share(value, slots, base):
        slots[here] = value
        copies = []
        for index, (y, z) in enumerate(plane):
            copy = remote(slots.at[here], slots.at[here], sem_p, base + index, device(y=y, z=z))
            copy.start()
            copies.append(copy)
        return copies

    def gather(copies, slots):
        for copy in copies:
            copy.wait()
        value = slots[0]
        for d in range(1, ngy * ngz):
            value = value + slots[d]
        return value

    def reduce(copies, own, slots):
        for d, copy in enumerate(copies):
            copy.wait()
            own = own + slots[d + 1]
        return own

    own = msg2[pl.ds(pl.multiple_of(dp * 8, 8), 8), :]
    share2 = share(reduce(scatter2, own, rz2), rp2, 0)
    share1 = share(reduce(scatter1, msg1[dp], rz1), rp1, len(plane))

    sums = gather(share2, rp2)
    main = exactly(sums, to_main)
    line = None
    for tap in range(8):
        row = main[tap : tap + 1]
        row = pltpu.roll(row, 3 * tap, 1) if tap else row
        line = row if line is None else line + row
    last = [exactly(sums, lanes) for lanes in to_last]
    for piece in range(3 * per2):
        row = last[piece // 8][piece % 8 : piece % 8 + 1]
        line = line + pltpu.roll(row, piece // 3 * NB * 27 + 24 + piece % 3, 1)
    out2[...] = line[0, : out2.shape[0]]
    line = gather(share1, rp1)
    for o in range(per1):
        out1[o * NC * 27 : (o + 1) * NC * 27] = line[0, o * L : o * L + NC * 27]


def shards(sizes, scales, volume, first, where_first, second, where_second, upstream, k1, k2):
    ndp, ngy, ngz = sizes
    k1 = jnp.transpose(k1, (2, 3, 4, 1, 0)).reshape(27, NC, NB)
    k2 = jnp.transpose(k2, (2, 3, 4, 1, 0)).reshape(27 * NB, NA)
    per2, per1 = NA // ndp, NB // ndp
    wide1 = per1 * L
    wide2 = pl.cdiv(per2 * 3 * NB + pl.cdiv(3 * per2, 8) * NB, L) * L
    there = ngy * ngz
    vmem = pl.BlockSpec(memory_space=pltpu.VMEM)
    grad_vol, first_out, second_out = pl.pallas_call(
        functools.partial(kernel, sizes, scales),
        out_shape=(
            jax.ShapeDtypeStruct((NC, FY, FZ, L), bf16),
            jax.ShapeDtypeStruct((per1 * NC * 27,), f32),
            jax.ShapeDtypeStruct((per2 * NB * 27,), f32),
        ),
        in_specs=[vmem] * 8,
        out_specs=(vmem,) * 3,
        scratch_shapes=[
            pltpu.VMEM(((HZ + 2) * NA, (HY + 2) * L), bf16),
            pltpu.VMEM(((FZ + 2) * NB, (FY + 2) * L), bf16),
            pltpu.VMEM((9 * HZ * NB, (HZ + 2) * NA), bf16),
            pltpu.VMEM((9 * NC * FZ, (FZ + 2) * NB), bf16),
            pltpu.VMEM((HZ * 3 * NB, HY * L), bf16),
            pltpu.VMEM((3 * NC * FZ + 2 * NB, (FY + 2) * L), bf16),
            pltpu.VMEM((2 * NB, FY * L), bf16),
            pltpu.VMEM((2, NC, FZ, L), bf16),
            pltpu.VMEM((9 * NA, L), f32),
            pltpu.VMEM((ndp, 1, wide1), f32),
            pltpu.VMEM((ndp * 8, wide2), f32),
            pltpu.VMEM((ndp, 1, wide1), f32),
            pltpu.VMEM((ndp, 8, wide2), f32),
            pltpu.VMEM((there, 1, wide1), f32),
            pltpu.VMEM((there, 8, wide2), f32),
            pltpu.SemaphoreType.DMA((2, 24)),
            pltpu.SemaphoreType.DMA((2, 2 * ndp)),
            pltpu.SemaphoreType.DMA((2, 2 * there)),
        ],
        compiler_params=pltpu.CompilerParams(collective_id=0, has_side_effects=True),
    )(
        volume[0],
        first[0],
        where_first[0],
        second[0, :, 0],
        where_second[0, :, 0],
        upstream[0, :, 0],
        k1,
        k2,
    )
    return (grad_vol[None], first_out, second_out)


def solution(mesh):
    sizes = tuple(mesh.shape[axis] for axis in ("dp", "gy", "gz"))
    cells = sizes[0] * sizes[1] * sizes[2] * FY * FZ * L
    scales = (math.sqrt(8.0 / cells), math.sqrt(64.0 / cells))
    split = P("dp", None, "gy", "gz", None)
    return jax.shard_map(
        functools.partial(shards, sizes, scales),
        mesh=mesh,
        in_specs=(split,) * 6 + (P(), P()),
        out_specs=(split, P("dp"), P("dp")),
        check_vma=False,
    )
```

time: 51.6 us -> 42.9 us (0.83)
  Pallas kernels: 47.2 us -> 39.4 us
  local copies, waits for them, and re-layouts: 3.46 us -> 2.59 us
    pallas_call x1, Pallas kernels: 47.2 us -> 39.4 us  [shards(): pl.pallas_call(functools.partial(kernel, sizes, scales), out_shape=(jax.S...]
    unnamed x5 -> x7, local copies, waits for them, and re-layouts: 0.73 us -> 2.59 us
    reshape x4 -> x0, local copies, waits for them, and re-layouts: 1.6 us -> none  [the longest x1 0.8 us: shards(): second_out = jnp.transpose(second_out, (2, 4, 0, 1, 3)).reshape(-1)]
    slice x1 -> x0, local copies, waits for them, and re-layouts: 0.77 us -> none  [shards(): sums[:, per2 * 3 * NB:(per2 * NB + per1 * NC) * 3]]
where the time goes in v2:
time: 42.9 us; the launch traced here: 42.7 us
  Pallas kernels  39.4 us (92%)
  local copies, waits for them, and re-layouts  2.59 us (6%)
  between operations  0.66 us (2%)
    pallas_call x1, Pallas kernels, shards(): pl.pallas_call(functools.partial(kernel, sizes, scales), out_shape=(jax.S...  39.4 us
    unnamed x7, local copies, waits for them, and re-layouts  2.59 us

profile of v2, /device:TPU:1, one launch (start us, length us, event | category | flops | bytes accessed | tf_op | source)
XLA Modules:
  0.0 42.7 jit_solution(4099258086799564781)
XLA Ops:
  0.6 39.4 %shard_map.103 = (bf16[4,4,16,128]{3,2,1,0:T(8,128)(2,1)}, f32[108]{0:T(128)}, f32[864]{0:T(1024)}) custom-call(bf16[4,4,16,128]{3,2,1,0:T(8,128)(2,1)} %bitcast.16, bf16[16,2,8,64]{3,2,1,0:T(8,128)(2,1)} %bitcast.17, s32[16,2,8,64]{3,2,1,0:T(8,128)} %bitcast.13, bf16[32,4,32]{2,1,0:T(4,128)(2,1)} %bitcast.19, s32[32,4,32]{2,1,0:T(4,128)} %bitcast.18, ...), custom_call_target="tpu_custom_call" | custom-call | tf_op jit(solution)/shard_map/pallas_call | solution.py:455
  40.1 0.0 copy-start.1
  40.1 0.0 copy-start
  40.1 1.5 %copy.14 = bf16[1,4,4,16,128]{4,3,2,1,0:T(8,128)(2,1)} copy(bf16[1,4,4,16,128]{4,3,2,1,0:T(8,128)(2,1)} %bitcast.15) | data formatting | bytes 131072
  41.6 0.0 copy-done.1
  41.6 0.5 %copy.15 = f32[108]{0:T(128)} copy(f32[108]{0:T(128)S(1)} %copy-done.1) | data formatting | bytes 864
  42.1 0.0 copy-done
  42.1 0.6 %copy.16 = f32[864]{0:T(1024)} copy(f32[864]{0:T(1024)S(1)} %copy-done) | data formatting | bytes 6912
Async XLA Ops:
  40.1 1.5 %copy-start.1 = (f32[108]{0:T(128)S(1)}, f32[108]{0:T(128)}, u32[]{:S(2)}) copy-start(f32[108]{0:T(128)} %get-tuple-element.13) | copy-start | bytes 1300
  40.1 2.0 %copy-start = (f32[864]{0:T(1024)S(1)}, f32[864]{0:T(1024)}, u32[]{:S(2)}) copy-start(f32[864]{0:T(1024)} %get-tuple-element.14) | copy-start | bytes 10372

commit v3 on v2

--- a/solution.py
+++ b/solution.py
@@ -80,6 +80,11 @@
     v3,
     vf,
     vh,
+    vz,
+    py,
+    pz,
+    qy,
+    qz,
     s2,
     msg1,
     msg2,
@@ -90,6 +95,7 @@
     sem_h,
     sem_z,
     sem_p,
+    sem_r,
 ):
     ndp, ngy, ngz = sizes
     per2, per1 = NA // ndp, NB // ndp
@@ -122,11 +128,19 @@
         ):
             field[row, col] = jnp.zeros_like(field[row, col])
     rows1 = 3 * NC * FZ
-    v3[rows1:, :] = jnp.zeros_like(v3[rows1:, :])
-    vh[...] = jnp.zeros_like(vh)
+    for field in (vh, vz, qy, qz):
+        field[...] = jnp.zeros_like(field)
     s2[...] = jnp.zeros_like(s2)
 
-    partners = [device(d=d) for d in range(1, ndp)] + [device(y=y, z=z) for y, z in plane]
+    partners = [dict(y=y, z=z) for y, z in around] + [dict(d=1), dict(d=-1)]
+    heard = [partners]
+    for step in range(1, rounds_of(sizes)):
+        far = []
+        for axis, count in (("d", ndp), ("y", ngy), ("z", ngz)):
+            if 2**step < count // 2:
+                far += [{axis: 2**step}, {axis: -(2**step)}]
+        heard.append(far)
+    partners = [device(**one) for one in partners]
     barrier = pltpu.get_barrier_semaphore()
     for one in partners:
         pl.semaphore_signal(barrier, inc=1, device_id=one, device_id_type=MESH)
@@ -140,14 +154,28 @@
     by4 = one_hot(iota((L // 4, L), 1) // 4 == iota((L // 4, L), 0))
     quarter = dot(quarter, by4)
     half_x = ((iota((NA, L), 1) // 2) % 2).astype(f32)
+    odd = iota((NA, L), 1) % 2 == 1
+    tiles = {}
     for z in range(HZ // 2):
         e = quarter[z * NA : (z + 1) * NA]
         w = quarter[(HZ // 2 + z) * NA : (HZ // 2 + z + 1) * NA] - half_x
         for dy in range(2):
             for dz in range(2):
-                tile = jnp.where(w == 4.0 * dy + 2.0 * dz, e, 0.0).astype(bf16)
+                tile = jnp.where(w == 4.0 * dy + 2.0 * dz, e, 0.0)
                 row, col = (2 * z + dz + 1) * NA, (dy + 1) * L
-                g2[row : row + NA, col : col + L] = tile
+                g2[row : row + NA, col : col + L] = tile.astype(bf16)
+                tiles[2 * z + dz, dy] = tile
+    for side, at_y, at_z in ((0, 0, 0), (1, HY - 1, HZ - 1)):
+        for z in range(HZ // 2):
+            pair = jnp.where(odd, tiles[2 * z + 1, at_y], tiles[2 * z, at_y])
+            py[side, z * NA : (z + 1) * NA] = pair.astype(bf16)
+        pz[side] = jnp.where(odd, tiles[at_z, 1], tiles[at_z, 0]).astype(bf16)
+
+    def unpaired(value):
+        value = value.astype(f32)
+        even_half = jnp.where(odd, pltpu.roll(value, 1, 1), value)
+        odd_half = jnp.where(odd, value, pltpu.roll(value, L - 1, 1))
+        return even_half.astype(bf16), odd_half.astype(bf16)
 
     def put_volume(here, i, col):
         for tx, by in enumerate((1, 0, -1)):
@@ -155,11 +183,11 @@
             v3[row : row + FZ, col : col + L] = (moved(here, by) if by else here).astype(bf16)
 
     for y in range(FY):
+        value = vol[:, y].astype(f32)
+        vf[0, y] = value[:, 0].astype(bf16)
+        vf[1, y] = value[:, FZ - 1].astype(bf16)
         for i in range(NC):
-            put_volume(vol[i, y].astype(f32), i, (y + 1) * L)
-    r, c = iota((2 * NB, rows1), 0), iota((2 * NB, rows1), 1)
-    sides = one_hot(c == (r % NB) * FZ + (r // NB) * (FZ - 1))
-    vf[...] = dot(sides, v3[:rows1, L : (FY + 1) * L]).astype(bf16)
+            put_volume(value[i], i, (y + 1) * L)
 
     by2 = one_hot(iota((L // 2, L), 1) // 2 == iota((L // 2, L), 0))
     halves = [first[:, y].astype(f32).reshape(NB * HZ, L // 2) for y in range(HY)]
@@ -195,7 +223,6 @@
 
     def rim(field, chans, ny, nz, base):
         copies = []
-        inner = {-1: (1, 1), 0: (1, None), 1: (None, 1)}
         for index, (y, z) in enumerate(around):
             height, width = (1 if z else nz), (1 if y else ny)
             from_row, to_row = (nz if z > 0 else 1), {-1: nz + 1, 0: 1, 1: 0}[z]
@@ -217,19 +244,42 @@
             if z == 0:
                 source, target = vol.at[:, FY - 1 if y > 0 else 0], vh.at[0 if y > 0 else 1]
             else:
-                from_col, to_col = (FY - 1 if y > 0 else 0), {-1: FY + 1, 0: 1, 1: 0}[y]
+                from_y, to_y = (FY - 1 if y > 0 else 0), {-1: FY + 1, 0: 1, 1: 0}[y]
                 width = 1 if y else FY
-                from_row, to_row = (NB if z > 0 else 0), rows1 + (0 if z > 0 else NB)
-                source = vf.at[pl.ds(from_row, NB), pl.ds(from_col * L, width * L)]
-                target = v3.at[pl.ds(to_row, NB), pl.ds(to_col * L, width * L)]
+                source = vf.at[1 if z > 0 else 0, pl.ds(from_y, width)]
+                target = vz.at[0 if z > 0 else 1, pl.ds(to_y, width)]
             copies.append(
                 ((y, z), remote(source, target, sem_h, base + index, device(y=y, z=z)))
             )
         return copies
 
-    rim2, rim_v = rim(g2, NA, HY, HZ, 0), volume_rim(8)
+    def paired_rim(base):
+        copies = []
+        for index, (y, z) in enumerate(around):
+            if y and z:
+                row, to_row = (HZ if z > 0 else 1), (0 if z > 0 else HZ + 1)
+                col, to_col = (HY if y > 0 else 1), (0 if y > 0 else HY + 1)
+                source = g2.at[pl.ds(row * NA, NA), pl.ds(col * L, L)]
+                target = g2.at[pl.ds(to_row * NA, NA), pl.ds(to_col * L, L)]
+            else:
+                up = 1 if y + z > 0 else 0
+                source, target = (py.at[up], qy.at[1 - up]) if y else (pz.at[up], qz.at[1 - up])
+            copies.append(
+                ((y, z), remote(source, target, sem_h, base + index, device(y=y, z=z)))
+            )
+        return copies
+
+    rim2, rim_v = paired_rim(0), volume_rim(8)
     start(rim2)
     start(rim_v)
+
+    def announce(step):
+        for one in heard[step]:
+            pl.semaphore_signal(
+                sem_r.at[step], inc=1, device_id=device(**one), device_id_type=MESH
+            )
+
+    announce(0)
 
     tiled = dot(k2[...], one_hot(iota((NA, (HZ + 2) * NA), 1) % NA == iota((NA, (HZ + 2) * NA), 0)))
     z_of = iota((NB, (HZ + 2) * NA), 1) // NA
@@ -268,7 +318,20 @@
                 row = ((ty * 3 + tx) * NC + i) * FZ
                 w1[row : row + FZ, :] = block.astype(bf16)
 
+    for step in range(len(heard)):
+        pl.semaphore_wait(sem_r.at[step], len(heard[step]))
+        if step + 1 < len(heard):
+            announce(step + 1)
+
     finish(rim2)
+    for side in range(2):
+        row, col = side * (HZ + 1) * NA, side * (HY + 1) * L
+        g2[row : row + NA, L : 2 * L], g2[row : row + NA, 2 * L : 3 * L] = unpaired(qz[side])
+        for z in range(HZ // 2):
+            low, high = unpaired(qy[side, z * NA : (z + 1) * NA])
+            row = (2 * z + 1) * NA
+            g2[row : row + NA, col : col + L] = low
+            g2[row + NA : row + 2 * NA, col : col + L] = high
 
     for ty in range(3):
         taps = None
@@ -344,6 +407,11 @@
     for side in range(2):
         for i in range(NC):
             put_volume(vh[side, i].astype(f32), i, side * (FY + 1) * L)
+        for y in range(FY + 2):
+            here = vz[side, y].astype(f32)
+            layers = [moved(here, 1), here, moved(here, -1), jnp.zeros_like(here)]
+            row = rows1 + side * NB
+            v3[row : row + NB, y * L : (y + 1) * L] = jnp.concatenate(layers, axis=0).astype(bf16)
 
     count = rows1 + 2 * NB
     c = iota((NB, count), 1)
@@ -443,6 +511,10 @@
         out1[o * NC * 27 : (o + 1) * NC * 27] = line[0, o * L : o * L + NC * 27]
 
 
+def rounds_of(sizes):
+    return max(1, (max(sizes) // 2 - 1).bit_length())
+
+
 def shards(sizes, scales, volume, first, where_first, second, where_second, upstream, k1, k2):
     ndp, ngy, ngz = sizes
     k1 = jnp.transpose(k1, (2, 3, 4, 1, 0)).reshape(27, NC, NB)
@@ -468,8 +540,13 @@
             pltpu.VMEM((9 * NC * FZ, (FZ + 2) * NB), bf16),
             pltpu.VMEM((HZ * 3 * NB, HY * L), bf16),
             pltpu.VMEM((3 * NC * FZ + 2 * NB, (FY + 2) * L), bf16),
-            pltpu.VMEM((2 * NB, FY * L), bf16),
+            pltpu.VMEM((2, FY, NC, L), bf16),
             pltpu.VMEM((2, NC, FZ, L), bf16),
+            pltpu.VMEM((2, FY + 2, NC, L), bf16),
+            pltpu.VMEM((2, HZ // 2 * NA, L), bf16),
+            pltpu.VMEM((2, NA, L), bf16),
+            pltpu.VMEM((2, HZ // 2 * NA, L), bf16),
+            pltpu.VMEM((2, NA, L), bf16),
             pltpu.VMEM((9 * NA, L), f32),
             pltpu.VMEM((ndp, 1, wide1), f32),
             pltpu.VMEM((ndp * 8, wide2), f32),
@@ -480,6 +557,7 @@
             pltpu.SemaphoreType.DMA((2, 24)),
             pltpu.SemaphoreType.DMA((2, 2 * ndp)),
             pltpu.SemaphoreType.DMA((2, 2 * there)),
+            pltpu.SemaphoreType.REGULAR((rounds_of(sizes),)),
         ],
         compiler_params=pltpu.CompilerParams(collective_id=0, has_side_effects=True),
     )(

time: 42.9 us -> 45 us (1.049)
  Pallas kernels: 39.4 us -> 41.5 us
    pallas_call x1, Pallas kernels: 39.4 us -> 41.5 us  [shards(): pl.pallas_call(functools.partial(kernel, sizes, scales), out_shape=(jax.S...]
where the time goes in v3:
time: 45 us; the launch traced here: 44.8 us
  Pallas kernels  41.5 us (92%)
  local copies, waits for them, and re-layouts  2.59 us (6%)
  between operations  0.66 us (1%)
    pallas_call x1, Pallas kernels, shards(): pl.pallas_call(functools.partial(kernel, sizes, scales), out_shape=(jax.S...  41.5 us
    unnamed x7, local copies, waits for them, and re-layouts  2.59 us

profile of v3, /device:TPU:1, one launch (start us, length us, event | category | flops | bytes accessed | tf_op | source)
XLA Modules:
  0.0 44.8 jit_solution(1024943620565999695)
XLA Ops:
  0.6 41.5 %shard_map.103 = (bf16[4,4,16,128]{3,2,1,0:T(8,128)(2,1)}, f32[108]{0:T(128)}, f32[864]{0:T(1024)}) custom-call(bf16[4,4,16,128]{3,2,1,0:T(8,128)(2,1)} %bitcast.16, bf16[16,2,8,64]{3,2,1,0:T(8,128)(2,1)} %bitcast.17, s32[16,2,8,64]{3,2,1,0:T(8,128)} %bitcast.13, bf16[32,4,32]{2,1,0:T(4,128)(2,1)} %bitcast.19, s32[32,4,32]{2,1,0:T(4,128)} %bitcast.18, ...), custom_call_target="tpu_custom_call" | custom-call | tf_op jit(solution)/shard_map/pallas_call | solution.py:527
  42.2 0.0 copy-start.1
  42.2 0.0 copy-start
  42.2 1.5 %copy.14 = bf16[1,4,4,16,128]{4,3,2,1,0:T(8,128)(2,1)} copy(bf16[1,4,4,16,128]{4,3,2,1,0:T(8,128)(2,1)} %bitcast.15) | data formatting | bytes 131072
  43.7 0.0 copy-done.1
  43.7 0.5 %copy.15 = f32[108]{0:T(128)} copy(f32[108]{0:T(128)S(1)} %copy-done.1) | data formatting | bytes 864
  44.2 0.0 copy-done
  44.2 0.6 %copy.16 = f32[864]{0:T(1024)} copy(f32[864]{0:T(1024)S(1)} %copy-done) | data formatting | bytes 6912
Async XLA Ops:
  42.2 1.5 %copy-start.1 = (f32[108]{0:T(128)S(1)}, f32[108]{0:T(128)}, u32[]{:S(2)}) copy-start(f32[108]{0:T(128)} %get-tuple-element.13) | copy-start | bytes 1300
  42.2 2.0 %copy-start = (f32[864]{0:T(1024)S(1)}, f32[864]{0:T(1024)}, u32[]{:S(2)}) copy-start(f32[864]{0:T(1024)} %get-tuple-element.14) | copy-start | bytes 10372

commit v4 on v3

--- a/solution.py
+++ b/solution.py
@@ -61,6 +61,23 @@
 def kernel(
     sizes,
     scales,
+    *refs,
+):
+    arguments, refs = refs[:8], refs[8:]
+    copied, refs = refs[-9:-1], refs[:-9] + refs[-1:]
+    loads = [
+        pltpu.make_async_copy(source, target, refs[-1].at[index])
+        for index, (source, target) in enumerate(zip(arguments, copied))
+    ]
+    for load in loads:
+        load.start()
+    body(sizes, scales, loads, *copied, *refs[:-1])
+
+
+def body(
+    sizes,
+    scales,
+    loads,
     vol,
     first,
     where_first,
@@ -132,19 +149,32 @@
         field[...] = jnp.zeros_like(field)
     s2[...] = jnp.zeros_like(s2)
 
-    partners = [dict(y=y, z=z) for y, z in around] + [dict(d=1), dict(d=-1)]
-    heard = [partners]
-    for step in range(1, rounds_of(sizes)):
+    partners = [device(y=y, z=z) for y, z in around] + [device(d=1), device(d=-1)]
+    along, across = rounds_of(sizes)
+    rounds = [[device(d=d) for d in (2**step, -(2**step))] for step in range(along)]
+    rounds += [[device(y=y, z=z) for y, z in around]]
+    for step in range(1, across):
         far = []
-        for axis, count in (("d", ndp), ("y", ngy), ("z", ngz)):
+        for axis, count in (("y", ngy), ("z", ngz)):
             if 2**step < count // 2:
-                far += [{axis: 2**step}, {axis: -(2**step)}]
-        heard.append(far)
-    partners = [device(**one) for one in partners]
+                far += [device(**{axis: 2**step}), device(**{axis: -(2**step)})]
+        rounds.append(far)
+
+    def announce(step):
+        for one in rounds[step]:
+            pl.semaphore_signal(sem_r.at[step], inc=1, device_id=one, device_id_type=MESH)
+
+    def hear(step):
+        pl.semaphore_wait(sem_r.at[step], len(rounds[step]))
+        if step + 1 not in (along, along + across):
+            announce(step + 1)
+
     barrier = pltpu.get_barrier_semaphore()
     for one in partners:
         pl.semaphore_signal(barrier, inc=1, device_id=one, device_id_type=MESH)
 
+    for load in loads[3:6]:
+        load.wait()
     upf = upstream[...].astype(f32)
     e2 = (upf * slope_of(second[...].astype(f32))).astype(bf16).astype(f32)
     p2 = where_second[...].astype(f32)
@@ -182,6 +212,7 @@
             row = (tx * NC + i) * FZ
             v3[row : row + FZ, col : col + L] = (moved(here, by) if by else here).astype(bf16)
 
+    loads[0].wait()
     for y in range(FY):
         value = vol[:, y].astype(f32)
         vf[0, y] = value[:, 0].astype(bf16)
@@ -189,6 +220,8 @@
         for i in range(NC):
             put_volume(value[i], i, (y + 1) * L)
 
+    for load in loads[1:3] + loads[6:]:
+        load.wait()
     by2 = one_hot(iota((L // 2, L), 1) // 2 == iota((L // 2, L), 0))
     halves = [first[:, y].astype(f32).reshape(NB * HZ, L // 2) for y in range(HY)]
     halves += [where_first[:, y].astype(f32).reshape(NB * HZ, L // 2) for y in range(HY)]
@@ -273,13 +306,8 @@
     start(rim2)
     start(rim_v)
 
-    def announce(step):
-        for one in heard[step]:
-            pl.semaphore_signal(
-                sem_r.at[step], inc=1, device_id=device(**one), device_id_type=MESH
-            )
-
     announce(0)
+    announce(along)
 
     tiled = dot(k2[...], one_hot(iota((NA, (HZ + 2) * NA), 1) % NA == iota((NA, (HZ + 2) * NA), 0)))
     z_of = iota((NB, (HZ + 2) * NA), 1) // NA
@@ -293,6 +321,7 @@
                 row = ((ty * 3 + tx) * HZ + z) * NB
                 w2[row : row + NB, :] = block.astype(bf16)
 
+    hear(0)
     for y in range(HY):
         here = act[:, y * L : (y + 1) * L]
         for tx, by in enumerate((2, 0, -2)):
@@ -301,6 +330,9 @@
                 row = (z * 3 + tx) * NB
                 a3[row : row + NB, y * L : (y + 1) * L] = value[z * NB : (z + 1) * NB]
 
+    for step in range(1, along - 1):
+        hear(step)
+    hear(along)
     width = (FZ + 2) * NB
     tiled = dot(
         k1[...].astype(f32).reshape(27 * NC, NB).astype(bf16),
@@ -318,11 +350,6 @@
                 row = ((ty * 3 + tx) * NC + i) * FZ
                 w1[row : row + FZ, :] = block.astype(bf16)
 
-    for step in range(len(heard)):
-        pl.semaphore_wait(sem_r.at[step], len(heard[step]))
-        if step + 1 < len(heard):
-            announce(step + 1)
-
     finish(rim2)
     for side in range(2):
         row, col = side * (HZ + 1) * NA, side * (HY + 1) * L
@@ -376,6 +403,8 @@
             copies.append(copy)
         return copies
 
+    if along > 1:
+        hear(along - 1)
     scatter2 = scatter(lambda k: msg2.at[pl.ds(pl.multiple_of(k * 8, 8), 8), :], rz2, 0)
 
     rows2 = 3 * HZ * NB
@@ -490,6 +519,8 @@
             own = own + slots[d + 1]
         return own
 
+    for step in range(1, across):
+        hear(along + step)
     own = msg2[pl.ds(pl.multiple_of(dp * 8, 8), 8), :]
     share2 = share(reduce(scatter2, own, rz2), rp2, 0)
     share1 = share(reduce(scatter1, msg1[dp], rz1), rp1, len(plane))
@@ -512,7 +543,7 @@
 
 
 def rounds_of(sizes):
-    return max(1, (max(sizes) // 2 - 1).bit_length())
+    return [max(1, (most // 2 - 1).bit_length()) for most in (sizes[0], max(sizes[1:]))]
 
 
 def shards(sizes, scales, volume, first, where_first, second, where_second, upstream, k1, k2):
@@ -524,6 +555,16 @@
     wide2 = pl.cdiv(per2 * 3 * NB + pl.cdiv(3 * per2, 8) * NB, L) * L
     there = ngy * ngz
     vmem = pl.BlockSpec(memory_space=pltpu.VMEM)
+    arguments = (
+        volume[0],
+        first[0],
+        where_first[0],
+        second[0, :, 0],
+        where_second[0, :, 0],
+        upstream[0, :, 0],
+        k1,
+        k2,
+    )
     grad_vol, first_out, second_out = pl.pallas_call(
         functools.partial(kernel, sizes, scales),
         out_shape=(
@@ -531,7 +572,7 @@
             jax.ShapeDtypeStruct((per1 * NC * 27,), f32),
             jax.ShapeDtypeStruct((per2 * NB * 27,), f32),
         ),
-        in_specs=[vmem] * 8,
+        in_specs=[pl.BlockSpec(memory_space=pltpu.HBM)] * 8,
         out_specs=(vmem,) * 3,
         scratch_shapes=[
             pltpu.VMEM(((HZ + 2) * NA, (HY + 2) * L), bf16),
@@ -557,19 +598,12 @@
             pltpu.SemaphoreType.DMA((2, 24)),
             pltpu.SemaphoreType.DMA((2, 2 * ndp)),
             pltpu.SemaphoreType.DMA((2, 2 * there)),
-            pltpu.SemaphoreType.REGULAR((rounds_of(sizes),)),
+            pltpu.SemaphoreType.REGULAR((sum(rounds_of(sizes)),)),
+            *[pltpu.VMEM(one.shape, one.dtype) for one in arguments],
+            pltpu.SemaphoreType.DMA((8,)),
         ],
         compiler_params=pltpu.CompilerParams(collective_id=0, has_side_effects=True),
-    )(
-        volume[0],
-        first[0],
-        where_first[0],
-        second[0, :, 0],
-        where_second[0, :, 0],
-        upstream[0, :, 0],
-        k1,
-        k2,
-    )
+    )(*arguments)
     return (grad_vol[None], first_out, second_out)
 
 

time: 45 us -> 40.6 us (0.902)
  Pallas kernels: 41.5 us -> 37.1 us
    pallas_call x1, Pallas kernels: 41.5 us -> 37.1 us  [shards(): pl.pallas_call(functools.partial(kernel, sizes, scales), out_shape=(jax.S...]
where the time goes in v4:
time: 40.6 us; the launch traced here: 40.4 us
  Pallas kernels  37.1 us (91%)
  local copies, waits for them, and re-layouts  2.59 us (6%)
  between operations  0.66 us (2%)
    pallas_call x1, Pallas kernels, shards(): pl.pallas_call(functools.partial(kernel, sizes, scales), out_shape=(jax.S...  37.1 us
    unnamed x7, local copies, waits for them, and re-layouts  2.59 us

profile of v4, /device:TPU:1, one launch (start us, length us, event | category | flops | bytes accessed | tf_op | source)
XLA Modules:
  0.0 40.4 jit_solution(16969453977689583618)
XLA Ops:
  0.6 37.1 %shard_map.103 = (bf16[4,4,16,128]{3,2,1,0:T(8,128)(2,1)}, f32[108]{0:T(128)}, f32[864]{0:T(1024)}) custom-call(bf16[4,4,16,128]{3,2,1,0:T(8,128)(2,1)} %bitcast.16, bf16[16,2,8,64]{3,2,1,0:T(8,128)(2,1)} %bitcast.17, s32[16,2,8,64]{3,2,1,0:T(8,128)} %bitcast.13, bf16[32,4,32]{2,1,0:T(4,128)(2,1)} %bitcast.19, s32[32,4,32]{2,1,0:T(4,128)} %bitcast.18, ...), custom_call_target="tpu_custom_call" | custom-call | tf_op jit(solution)/shard_map/pallas_call | solution.py:568
  37.8 0.0 copy-start.1
  37.8 0.0 copy-start
  37.8 1.5 %copy.14 = bf16[1,4,4,16,128]{4,3,2,1,0:T(8,128)(2,1)} copy(bf16[1,4,4,16,128]{4,3,2,1,0:T(8,128)(2,1)} %bitcast.15) | data formatting | bytes 131072
  39.3 0.0 copy-done.1
  39.3 0.5 %copy.15 = f32[108]{0:T(128)} copy(f32[108]{0:T(128)S(1)} %copy-done.1) | data formatting | bytes 864
  39.8 0.0 copy-done
  39.8 0.6 %copy.16 = f32[864]{0:T(1024)} copy(f32[864]{0:T(1024)S(1)} %copy-done) | data formatting | bytes 6912
Async XLA Ops:
  37.8 1.5 %copy-start.1 = (f32[108]{0:T(128)S(1)}, f32[108]{0:T(128)}, u32[]{:S(2)}) copy-start(f32[108]{0:T(128)} %get-tuple-element.13) | copy-start | bytes 1300
  37.8 2.0 %copy-start = (f32[864]{0:T(1024)S(1)}, f32[864]{0:T(1024)}, u32[]{:S(2)}) copy-start(f32[864]{0:T(1024)} %get-tuple-element.14) | copy-start | bytes 10372

commit v5 on v4

--- a/solution.py
+++ b/solution.py
@@ -127,6 +127,12 @@
     around = [(y, z) for y in (-1, 0, 1) for z in (-1, 0, 1) if (y, z) != (0, 0)]
     plane = [(y, z) for y in range(ngy) for z in range(ngz) if (y, z) != (0, 0)]
 
+    def hops(y, z):
+        return min(z, ngz - z) * 2 + min(y, ngy - y)
+
+    plane = sorted(plane, key=lambda one: -hops(*one))
+    distances = sorted(range(1, ndp), key=lambda d: -min(d, ndp - d))
+
     def exists(y, z):
         on = None
         for step, index, count in ((y, gy, ngy), (z, gz, ngz)):
@@ -149,25 +155,11 @@
         field[...] = jnp.zeros_like(field)
     s2[...] = jnp.zeros_like(s2)
 
-    partners = [device(y=y, z=z) for y, z in around] + [device(d=1), device(d=-1)]
-    along, across = rounds_of(sizes)
-    rounds = [[device(d=d) for d in (2**step, -(2**step))] for step in range(along)]
-    rounds += [[device(y=y, z=z) for y, z in around]]
-    for step in range(1, across):
-        far = []
-        for axis, count in (("y", ngy), ("z", ngz)):
-            if 2**step < count // 2:
-                far += [device(**{axis: 2**step}), device(**{axis: -(2**step)})]
-        rounds.append(far)
-
-    def announce(step):
-        for one in rounds[step]:
-            pl.semaphore_signal(sem_r.at[step], inc=1, device_id=one, device_id_type=MESH)
-
-    def hear(step):
-        pl.semaphore_wait(sem_r.at[step], len(rounds[step]))
-        if step + 1 not in (along, along + across):
-            announce(step + 1)
+    near = reach(ndp)
+    close = [(y % ngy, z % ngz) for y, z in around]
+    partners = [device(y=y, z=z) for y, z in sorted(plane, key=lambda one: one not in close)]
+    partners += [device(d=sign * d) for d in range(near, 0, -1) for sign in (1, -1)]
+    rim_dp = [device(d=near), device(d=-near)] if near < ndp // 2 else []
 
     barrier = pltpu.get_barrier_semaphore()
     for one in partners:
@@ -207,32 +199,6 @@
         odd_half = jnp.where(odd, value, pltpu.roll(value, L - 1, 1))
         return even_half.astype(bf16), odd_half.astype(bf16)
 
-    def put_volume(here, i, col):
-        for tx, by in enumerate((1, 0, -1)):
-            row = (tx * NC + i) * FZ
-            v3[row : row + FZ, col : col + L] = (moved(here, by) if by else here).astype(bf16)
-
-    loads[0].wait()
-    for y in range(FY):
-        value = vol[:, y].astype(f32)
-        vf[0, y] = value[:, 0].astype(bf16)
-        vf[1, y] = value[:, FZ - 1].astype(bf16)
-        for i in range(NC):
-            put_volume(value[i], i, (y + 1) * L)
-
-    for load in loads[1:3] + loads[6:]:
-        load.wait()
-    by2 = one_hot(iota((L // 2, L), 1) // 2 == iota((L // 2, L), 0))
-    halves = [first[:, y].astype(f32).reshape(NB * HZ, L // 2) for y in range(HY)]
-    halves += [where_first[:, y].astype(f32).reshape(NB * HZ, L // 2) for y in range(HY)]
-    halves = [dot(each.astype(bf16), by2).astype(bf16) for each in halves]
-    r, c = iota((NB * HZ, NB * HZ), 0), iota((NB * HZ, NB * HZ), 1)
-    order = one_hot(c == (r % NB) * HZ + r // NB)
-    halves = dot(order, jnp.concatenate(halves, axis=1))
-    pre1, p1 = halves[:, : HY * L], halves[:, HY * L :]
-    slope1 = slope_of(pre1)
-    act = jnp.where(pre1 > 0, pre1, LEAK * pre1).astype(bf16).astype(f32)
-
     pl.semaphore_wait(barrier, len(partners))
 
     def remote(src, dst, sems, index, to):
@@ -304,10 +270,36 @@
 
     rim2, rim_v = paired_rim(0), volume_rim(8)
     start(rim2)
+    for one in rim_dp:
+        pl.semaphore_signal(sem_r.at[0], inc=1, device_id=one, device_id_type=MESH)
+    loads[0].wait()
+    for y in range(FY):
+        value = vol[:, y].astype(f32)
+        vf[0, y] = value[:, 0].astype(bf16)
+        vf[1, y] = value[:, FZ - 1].astype(bf16)
     start(rim_v)
 
-    announce(0)
-    announce(along)
+    def put_volume(here, i, col):
+        for tx, by in enumerate((1, 0, -1)):
+            row = (tx * NC + i) * FZ
+            v3[row : row + FZ, col : col + L] = (moved(here, by) if by else here).astype(bf16)
+
+    for y in range(FY):
+        for i in range(NC):
+            put_volume(vol[i, y].astype(f32), i, (y + 1) * L)
+
+    for load in loads[1:3] + loads[6:]:
+        load.wait()
+    by2 = one_hot(iota((L // 2, L), 1) // 2 == iota((L // 2, L), 0))
+    halves = [first[:, y].astype(f32).reshape(NB * HZ, L // 2) for y in range(HY)]
+    halves += [where_first[:, y].astype(f32).reshape(NB * HZ, L // 2) for y in range(HY)]
+    halves = [dot(each.astype(bf16), by2).astype(bf16) for each in halves]
+    r, c = iota((NB * HZ, NB * HZ), 0), iota((NB * HZ, NB * HZ), 1)
+    order = one_hot(c == (r % NB) * HZ + r // NB)
+    halves = dot(order, jnp.concatenate(halves, axis=1))
+    pre1, p1 = halves[:, : HY * L], halves[:, HY * L :]
+    slope1 = slope_of(pre1)
+    act = jnp.where(pre1 > 0, pre1, LEAK * pre1).astype(bf16).astype(f32)
 
     tiled = dot(k2[...], one_hot(iota((NA, (HZ + 2) * NA), 1) % NA == iota((NA, (HZ + 2) * NA), 0)))
     z_of = iota((NB, (HZ + 2) * NA), 1) // NA
@@ -321,7 +313,6 @@
                 row = ((ty * 3 + tx) * HZ + z) * NB
                 w2[row : row + NB, :] = block.astype(bf16)
 
-    hear(0)
     for y in range(HY):
         here = act[:, y * L : (y + 1) * L]
         for tx, by in enumerate((2, 0, -2)):
@@ -330,9 +321,6 @@
                 row = (z * 3 + tx) * NB
                 a3[row : row + NB, y * L : (y + 1) * L] = value[z * NB : (z + 1) * NB]
 
-    for step in range(1, along - 1):
-        hear(step)
-    hear(along)
     width = (FZ + 2) * NB
     tiled = dot(
         k1[...].astype(f32).reshape(27 * NC, NB).astype(bf16),
@@ -397,14 +385,14 @@
 
     def scatter(message, slots, base):
         copies = []
-        for d in range(1, ndp):
+        for d in distances:
             copy = remote(message(at(dp, d, ndp)), slots.at[d], sem_z, base + d, device(d=d))
             copy.start()
             copies.append(copy)
         return copies
 
-    if along > 1:
-        hear(along - 1)
+    if rim_dp:
+        pl.semaphore_wait(sem_r.at[0], len(rim_dp))
     scatter2 = scatter(lambda k: msg2.at[pl.ds(pl.multiple_of(k * 8, 8), 8), :], rz2, 0)
 
     rows2 = 3 * HZ * NB
@@ -514,13 +502,12 @@
         return value
 
     def reduce(copies, own, slots):
-        for d, copy in enumerate(copies):
+        for copy in copies:
             copy.wait()
-            own = own + slots[d + 1]
+        for d in range(1, ndp):
+            own = own + slots[d]
         return own
 
-    for step in range(1, across):
-        hear(along + step)
     own = msg2[pl.ds(pl.multiple_of(dp * 8, 8), 8), :]
     share2 = share(reduce(scatter2, own, rz2), rp2, 0)
     share1 = share(reduce(scatter1, msg1[dp], rz1), rp1, len(plane))
@@ -542,8 +529,13 @@
         out1[o * NC * 27 : (o + 1) * NC * 27] = line[0, o * L : o * L + NC * 27]
 
 
-def rounds_of(sizes):
-    return [max(1, (most // 2 - 1).bit_length()) for most in (sizes[0], max(sizes[1:]))]
+def reach(ndp):
+    return max(1, ndp // 4)
+
+
+def handed_on(*refs):
+    for source, target in zip(refs[:3], refs[3:]):
+        target[...] = source[...]
 
 
 def shards(sizes, scales, volume, first, where_first, second, where_second, upstream, k1, k2):
@@ -565,7 +557,7 @@
         k1,
         k2,
     )
-    grad_vol, first_out, second_out = pl.pallas_call(
+    results = pl.pallas_call(
         functools.partial(kernel, sizes, scales),
         out_shape=(
             jax.ShapeDtypeStruct((NC, FY, FZ, L), bf16),
@@ -598,12 +590,19 @@
             pltpu.SemaphoreType.DMA((2, 24)),
             pltpu.SemaphoreType.DMA((2, 2 * ndp)),
             pltpu.SemaphoreType.DMA((2, 2 * there)),
-            pltpu.SemaphoreType.REGULAR((sum(rounds_of(sizes)),)),
+            pltpu.SemaphoreType.REGULAR((1,)),
             *[pltpu.VMEM(one.shape, one.dtype) for one in arguments],
             pltpu.SemaphoreType.DMA((8,)),
         ],
         compiler_params=pltpu.CompilerParams(collective_id=0, has_side_effects=True),
     )(*arguments)
+    grad_vol, first_out, second_out = pl.pallas_call(
+        handed_on,
+        out_shape=tuple(jax.ShapeDtypeStruct(one.shape, one.dtype) for one in results),
+        in_specs=[vmem] * 3,
+        out_specs=(vmem,) * 3,
+
+    )(*results)
     return (grad_vol[None], first_out, second_out)
 
 

time: 40.6 us -> 39.2 us (0.966)
  local copies, waits for them, and re-layouts: 2.59 us -> 0 us
  Pallas kernels: 37.1 us -> 38.4 us
    unnamed x7 -> x0, local copies, waits for them, and re-layouts: 2.59 us -> none
    pallas_call x0 -> x1, Pallas kernels: none -> 1.48 us  [shards(): pl.pallas_call(handed_on, out_shape=tuple((jax.ShapeDtypeStruct(one.shape...]
where the time goes in v5:
time: 39.2 us; the launch traced here: 39 us
  Pallas kernels  38.4 us (98%)
  between operations  0.64 us (2%)
    pallas_call x1, Pallas kernels, shards(): pl.pallas_call(functools.partial(kernel, sizes, scales), out_shape=(jax.S...  36.9 us
    pallas_call x1, Pallas kernels, shards(): pl.pallas_call(handed_on, out_shape=tuple((jax.ShapeDtypeStruct(one.shape...  1.48 us

profile of v5, /device:TPU:1, one launch (start us, length us, event | category | flops | bytes accessed | tf_op | source)
XLA Modules:
  0.0 39.0 jit_solution(4842535290118244026)
XLA Ops:
  0.6 36.9 %shard_map.103 = (bf16[4,4,16,128]{3,2,1,0:T(8,128)(2,1)}, f32[108]{0:T(128)}, f32[864]{0:T(1024)}) custom-call(bf16[4,4,16,128]{3,2,1,0:T(8,128)(2,1)} %bitcast.15, bf16[16,2,8,64]{3,2,1,0:T(8,128)(2,1)} %bitcast.16, s32[16,2,8,64]{3,2,1,0:T(8,128)} %bitcast.13, bf16[32,4,32]{2,1,0:T(4,128)(2,1)} %bitcast.18, s32[32,4,32]{2,1,0:T(4,128)} %bitcast.17, ...), custom_call_target="tpu_custom_call" | custom-call | tf_op jit(solution)/shard_map/pallas_call | solution.py:560
  37.5 1.5 %shard_map.104 = (bf16[4,4,16,128]{3,2,1,0:T(8,128)(2,1)}, f32[108]{0:T(128)}, f32[864]{0:T(1024)}) custom-call(bf16[4,4,16,128]{3,2,1,0:T(8,128)(2,1)} %get-tuple-element.9.refs_0_, f32[108]{0:T(128)} %get-tuple-element.10.refs_1_, f32[864]{0:T(1024)} %get-tuple-element.11.refs_2_), custom_call_target="tpu_custom_call" | custom-call | tf_op jit(solution)/shard_map/pallas_call | solution.py:599

commit v6 on v5

--- a/solution.py
+++ b/solution.py
@@ -69,7 +69,7 @@
         pltpu.make_async_copy(source, target, refs[-1].at[index])
         for index, (source, target) in enumerate(zip(arguments, copied))
     ]
-    for load in loads:
+    for load in loads[3:6] + loads[:3] + loads[6:]:
         load.start()
     body(sizes, scales, loads, *copied, *refs[:-1])
 
@@ -156,8 +156,13 @@
     s2[...] = jnp.zeros_like(s2)
 
     near = reach(ndp)
-    close = [(y % ngy, z % ngz) for y, z in around]
-    partners = [device(y=y, z=z) for y, z in sorted(plane, key=lambda one: one not in close)]
+    partners = [device(y=y, z=z) for y, z in around]
+    far = [device(z=2), device(z=-2)] if 2 < ngz // 2 else []
+
+    def tell(step, those):
+        for one in those:
+            pl.semaphore_signal(sem_r.at[step], inc=1, device_id=one, device_id_type=MESH)
+
     partners += [device(d=sign * d) for d in range(near, 0, -1) for sign in (1, -1)]
     rim_dp = [device(d=near), device(d=-near)] if near < ndp // 2 else []
 
@@ -270,8 +275,8 @@
 
     rim2, rim_v = paired_rim(0), volume_rim(8)
     start(rim2)
-    for one in rim_dp:
-        pl.semaphore_signal(sem_r.at[0], inc=1, device_id=one, device_id_type=MESH)
+    tell(0, rim_dp)
+    tell(1, [device(y=y, z=z) for y, z in around])
     loads[0].wait()
     for y in range(FY):
         value = vol[:, y].astype(f32)
@@ -339,6 +344,8 @@
                 w1[row : row + FZ, :] = block.astype(bf16)
 
     finish(rim2)
+    pl.semaphore_wait(sem_r.at[1], len(around))
+    tell(2, far)
     for side in range(2):
         row, col = side * (HZ + 1) * NA, side * (HY + 1) * L
         g2[row : row + NA, L : 2 * L], g2[row : row + NA, 2 * L : 3 * L] = unpaired(qz[side])
@@ -508,6 +515,8 @@
             own = own + slots[d]
         return own
 
+    if far:
+        pl.semaphore_wait(sem_r.at[2], len(far))
     own = msg2[pl.ds(pl.multiple_of(dp * 8, 8), 8), :]
     share2 = share(reduce(scatter2, own, rz2), rp2, 0)
     share1 = share(reduce(scatter1, msg1[dp], rz1), rp1, len(plane))
@@ -534,8 +543,16 @@
 
 
 def handed_on(*refs):
-    for source, target in zip(refs[:3], refs[3:]):
-        target[...] = source[...]
+    sources, targets, held, sems = refs[:3], refs[3:6], refs[6:9], refs[9]
+    loads = [pltpu.make_async_copy(sources[n], held[n], sems.at[0, n]) for n in range(3)]
+    stores = [pltpu.make_async_copy(held[n], targets[n], sems.at[1, n]) for n in range(3)]
+    for load in loads:
+        load.start()
+    for load, store in zip(loads, stores):
+        load.wait()
+        store.start()
+    for store in stores:
+        store.wait()
 
 
 def shards(sizes, scales, volume, first, where_first, second, where_second, upstream, k1, k2):
@@ -590,7 +607,7 @@
             pltpu.SemaphoreType.DMA((2, 24)),
             pltpu.SemaphoreType.DMA((2, 2 * ndp)),
             pltpu.SemaphoreType.DMA((2, 2 * there)),
-            pltpu.SemaphoreType.REGULAR((1,)),
+            pltpu.SemaphoreType.REGULAR((3,)),
             *[pltpu.VMEM(one.shape, one.dtype) for one in arguments],
             pltpu.SemaphoreType.DMA((8,)),
         ],
@@ -599,8 +616,10 @@
     grad_vol, first_out, second_out = pl.pallas_call(
         handed_on,
         out_shape=tuple(jax.ShapeDtypeStruct(one.shape, one.dtype) for one in results),
-        in_specs=[vmem] * 3,
-        out_specs=(vmem,) * 3,
+        in_specs=[pl.BlockSpec(memory_space=pltpu.HBM)] * 3,
+        out_specs=(pl.BlockSpec(memory_space=pltpu.HBM),) * 3,
+        scratch_shapes=[pltpu.VMEM(one.shape, one.dtype) for one in results]
+        + [pltpu.SemaphoreType.DMA((2, 3))],
 
     )(*results)
     return (grad_vol[None], first_out, second_out)

time: 39.2 us -> 38.3 us (0.977)
  Pallas kernels: 38.4 us -> 37.5 us
    pallas_call x1, Pallas kernels: 36.9 us -> 36 us  [shards(): pl.pallas_call(functools.partial(kernel, sizes, scales), out_shape=(jax.S...]
where the time goes in v6:
time: 38.3 us; the launch traced here: 38.1 us
  Pallas kernels  37.5 us (98%)
  between operations  0.64 us (2%)
    pallas_call x1, Pallas kernels, shards(): pl.pallas_call(functools.partial(kernel, sizes, scales), out_shape=(jax.S...  36 us
    pallas_call x1, Pallas kernels, shards(): pl.pallas_call(handed_on, out_shape=tuple((jax.ShapeDtypeStruct(one.shape...  1.53 us

profile of v6, /device:TPU:1, one launch (start us, length us, event | category | flops | bytes accessed | tf_op | source)
XLA Modules:
  0.0 38.1 jit_solution(8604299633823462230)
XLA Ops:
  0.6 36.0 %shard_map.103 = (bf16[4,4,16,128]{3,2,1,0:T(8,128)(2,1)}, f32[108]{0:T(128)}, f32[864]{0:T(1024)}) custom-call(bf16[4,4,16,128]{3,2,1,0:T(8,128)(2,1)} %bitcast.15, bf16[16,2,8,64]{3,2,1,0:T(8,128)(2,1)} %bitcast.16, s32[16,2,8,64]{3,2,1,0:T(8,128)} %bitcast.13, bf16[32,4,32]{2,1,0:T(4,128)(2,1)} %bitcast.18, s32[32,4,32]{2,1,0:T(4,128)} %bitcast.17, ...), custom_call_target="tpu_custom_call" | custom-call | tf_op jit(solution)/shard_map/pallas_call | solution.py:577
  36.6 1.5 %shard_map.104 = (bf16[4,4,16,128]{3,2,1,0:T(8,128)(2,1)}, f32[108]{0:T(128)}, f32[864]{0:T(1024)}) custom-call(bf16[4,4,16,128]{3,2,1,0:T(8,128)(2,1)} %get-tuple-element.9.refs_0_, f32[108]{0:T(128)} %get-tuple-element.10.refs_1_, f32[864]{0:T(1024)} %get-tuple-element.11.refs_2_), custom_call_target="tpu_custom_call" | custom-call | tf_op jit(solution)/shard_map/pallas_call | solution.py:616
